TPU v7x, 32 devices: a whole 2x2x4 slice. The times are simulated.
32 devices in a mesh: src: 4 (over z), dst: 8 (over y, x, core).
Axes of the slice: x: 2, y: 2, z: 4, core: 2. Of those that a mesh axis runs over, the one named last changes fastest.
Arguments:
- src_emb: bfloat16 [65536, 128], P('src'), may hold values from -1.5 to 1.5
- dst_emb: bfloat16 [65536, 128], P('dst'), may hold values from -1.5 to 1.5
- out_emb: bfloat16 [65536, 128], P('dst'), may hold values from -1.5 to 1.5
- word_table: bfloat16 [32768, 128], P('dst'), may hold values from -1.5 to 1.5
- log_norm: float32 [65536], P('dst'), may hold values from 9 to 11
- block_mask: int32 [128, 128], P('src', 'dst'), may hold values from 0 to 1, as said below
- tokens: int32 [3, 8], replicated, may hold values from 0 to 32767
- alpha_start: float32 [8, 65536], P(None, 'src'), may hold values from 0.5 to 80
- beta_end: float32 [8, 65536], P(None, 'dst'), may hold values from 0.5 to 80
Outputs:
- alpha_end: float32 [8, 65536], P(None, 'dst')
- beta_start: float32 [8, 65536], P(None, 'src')
- block_counts: float32 [128, 128], P('src', 'dst')
Inputs may be any that keep to these rules, and one draw needn't show every extreme that they name: block_mask[I, I] = 1 for every block I: a state may always move within its own block.
All inputs are finite; a program needn't handle non-finite values.
Results may differ from a plain program's by a relative error of at most 0.0032.
Values may be sent and summed in bfloat16 or wider, within the bound.
A program may use at most 384 MiB of HBM per device.

v0:
```python
import jax
import jax.numpy as jnp
from jax import lax
from jax.sharding import PartitionSpec as P

BLK = 512
STEPS = 3
NB = 128


very_negative = -1e30


def joined(array, axis, combine):
    everything = jax.tree.map(lambda part: lax.all_gather(part, axis), array)
    initial = jax.tree.map(lambda part: part[0], everything)

    def step(k, so_far):
        return combine(so_far, jax.tree.map(lambda part: part[k], everything))

    return lax.fori_loop(1, lax.axis_size(axis), step, initial)


def local(
    src_emb, dst_emb, out_emb, word_table, log_norm, block_mask, tokens, alpha_start, beta_end
):
    row_count = src_emb.shape[0]
    col_count = dst_emb.shape[0]
    emb_width = src_emb.shape[1]
    row_blocks = row_count // BLK
    col_blocks = col_count // BLK
    traces = alpha_start.shape[0]
    src_count = lax.axis_size("src")
    states = row_count * src_count
    src_place = lax.axis_index("src")
    dst_place = lax.axis_index("dst")
    vocab_slice = word_table.shape[0]
    local_ids = tokens.reshape(-1) - dst_place * vocab_slice
    onehot = (local_ids[:, None] == jnp.arange(vocab_slice, dtype=jnp.int32)[None, :]).astype(
        jnp.bfloat16
    )
    looked = jnp.dot(onehot, word_table, preferred_element_type=jnp.float32)
    word_rows = lax.psum(looked.astype(jnp.bfloat16), "dst")
    logits = lax.dot_general(
        word_rows, out_emb, (((1,), (1,)), ((), ())), preferred_element_type=jnp.float32
    )
    emission = jnp.exp(logits - log_norm[None, :]).reshape(STEPS, traces, col_count)

    def table_block(running, inputs):
        src_rows, mask_row = inputs
        scores = lax.dot_general(
            src_rows, dst_emb, (((1,), (1,)), ((), ())), preferred_element_type=jnp.float32
        )
        scores = scores.reshape(BLK, col_blocks, BLK)
        block_top = jnp.max(scores, axis=2)
        block_sum = jnp.sum(jnp.exp(scores - block_top[:, :, None]), axis=2)
        allowed = (mask_row == 1)[None, :]
        row_best = jnp.max(jnp.where(allowed, block_top, very_negative), axis=1)
        row_mass = jnp.sum(
            jnp.where(allowed, block_sum * jnp.exp(block_top - row_best[:, None]), 0.0), axis=1
        )
        transit = jnp.where(
            allowed[:, :, None], jnp.exp(scores - block_top[:, :, None]), 0.0
        ).astype(jnp.bfloat16)
        return (running, (block_top.T, row_best, row_mass, transit))

    _, (block_top, row_best, row_mass, transit) = lax.scan(
        table_block, 0, (src_emb.reshape(row_blocks, BLK, emb_width), block_mask)
    )
    row_best = row_best.reshape(row_count)
    row_mass = row_mass.reshape(row_count)

    def combine(left_pair, right_pair):
        joint = jnp.maximum(left_pair[0], right_pair[0])
        return (
            joint,
            left_pair[1] * jnp.exp(left_pair[0] - joint)
            + right_pair[1] * jnp.exp(right_pair[0] - joint),
        )

    whole_best, whole_mass = joined((row_best, row_mass), "dst", combine)
    log_total = (whole_best + jnp.log(whole_mass)).reshape(row_blocks, 1, BLK)
    factor = jnp.where(block_mask[:, :, None] == 1, jnp.exp(block_top - log_total), 0.0)

    def forward_finish(partial_value, scale, position, final):
        predicted = lax.psum(partial_value, "src")
        alpha_cols = predicted * emission[position] / scale[:, None]
        if final:
            return (alpha_cols, alpha_cols)
        gathered = lax.all_gather(alpha_cols, "dst", axis=1, tiled=True)
        alpha_rows = lax.dynamic_slice_in_dim(gathered, src_place * row_count, row_count, 1)
        return (alpha_rows, alpha_cols)

    def backward_finish(partial_value, scale, final):
        beta_rows = lax.psum(partial_value, "dst") / scale[:, None]
        if final:
            return (beta_rows, beta_rows)
        gathered = lax.all_gather(beta_rows, "src", axis=1, tiled=True)
        beta_cols = lax.dynamic_slice_in_dim(gathered, dst_place * col_count, col_count, 1)
        return (beta_rows, beta_cols)

    mix_store = [None] * STEPS
    spread_store = [None] * STEPS
    alpha_rows = alpha_start
    alpha_cols = None
    beta_rows = None
    beta_cols = beta_end
    for k in range(STEPS):
        mix_terms = (alpha_rows.reshape(traces, row_blocks, 1, BLK) * factor[None]).astype(
            jnp.bfloat16
        )
        forward_partial_value = jnp.einsum(
            "bijr,irjc->bjc", mix_terms, transit, preferred_element_type=jnp.float32
        )
        forward_partial_value = forward_partial_value.reshape(traces, col_count)
        mix_terms, forward_partial, forward_scale = (
            mix_terms,
            forward_partial_value,
            jnp.sum(forward_partial_value * emission[k], axis=1),
        )
        mix_store[k] = mix_terms
        forward_total = lax.psum(forward_scale, ("src", "dst"))
        alpha_rows, alpha_cols = forward_finish(
            forward_partial, forward_total / states, k, k == STEPS - 1
        )
    for k in range(STEPS):
        mirror = STEPS - 1 - k
        weights = (
            (emission[mirror] * beta_cols).astype(jnp.bfloat16).reshape(traces, col_blocks, BLK)
        )
        spread = jnp.einsum("irjc,bjc->bijr", transit, weights, preferred_element_type=jnp.float32)
        backward_partial_value = jnp.sum(factor[None] * spread, axis=2).reshape(traces, row_count)
        spread, backward_partial, backward_scale = (
            spread,
            backward_partial_value,
            jnp.sum(backward_partial_value, axis=1),
        )
        spread_store[mirror] = spread
        backward_total = lax.psum(backward_scale, ("src", "dst"))
        beta_rows, beta_cols = backward_finish(
            backward_partial, backward_total / states, mirror == 0
        )
    block_terms = jnp.stack(
        [jnp.sum(mix_store[t].astype(jnp.float32) * spread_store[t], axis=3) for t in range(STEPS)]
    )
    pair_total = lax.psum(jnp.sum(block_terms, axis=(2, 3)), ("src", "dst"))
    counts = jnp.sum(block_terms / pair_total[:, :, None, None], axis=(0, 1)) * (
        NB * NB / (STEPS * traces)
    )
    return (alpha_cols, beta_rows, counts)


def solution(mesh):
    return jax.shard_map(
        local,
        mesh=mesh,
        in_specs=(
            P("src", None),
            P("dst", None),
            P("dst", None),
            P("dst", None),
            P("dst"),
            P("src", "dst"),
            P(),
            P(None, "src"),
            P(None, "dst"),
        ),
        out_specs=(P(None, "dst"), P(None, "src"), P("src", "dst")),
        check_vma=False,
    )
```

profile of v0, /device:TPU:0, one launch (start us, length us, event | category | flops | bytes accessed | tf_op | source)
XLA Modules:
  0.0 1764.3 jit_solution(14703799814664994495)
XLA Ops:
  8.1 765.1 %while.35 = (s32[]{:T(128)}, f32[32,16,512]{2,1,0:T(8,128)}, f32[32,512]{1,0:T(8,128)S(1)}, f32[32,512]{1,0:T(8,128)S(1)}, bf16[32,512,16,512]{1,3,2,0:T(8,128)(...) while((s32[]{:T(128)}, f32[32,16,512]{2,1,0:T(8,128)}, ...), condition=%wide.region_5.6_spmd.clone, body=%wide.region_0.5_spmd.sunk.clone | while | flops 1098939392 | bytes 128368376 | solution.py:67
  12.2 5.7 copy-done.1
  22.9 8.3 fusion.58
  36.1 5.7 copy-done.1
  46.8 8.3 fusion.58
  70.8 8.3 fusion.58
  94.7 8.3 fusion.58
  108.0 5.7 copy-done.1
  118.6 8.3 fusion.58
  142.6 8.3 fusion.58
  166.5 8.3 fusion.58
  179.7 5.7 copy-done.1
  190.4 8.3 fusion.58
  203.6 5.7 copy-done.1
  214.2 8.3 fusion.58
  227.5 5.7 copy-done.1
  238.1 8.3 fusion.58
  251.4 5.7 copy-done.1
  262.0 8.3 fusion.58
  275.3 5.7 copy-done.1
  285.9 8.3 fusion.58
  309.8 8.3 fusion.58
  323.1 5.7 copy-done.1
  333.7 8.3 fusion.58
  357.6 8.3 fusion.58
  381.5 8.3 fusion.58
  405.4 8.3 fusion.58
  429.4 8.3 fusion.58
  453.3 8.3 fusion.58
  477.3 8.3 fusion.58
  501.2 8.3 fusion.58
  525.1 8.3 fusion.58
  549.0 8.3 fusion.58
  572.9 8.3 fusion.58
  596.8 8.3 fusion.58
  620.7 8.3 fusion.58
  644.6 8.3 fusion.58
  668.5 8.3 fusion.58
  692.4 8.3 fusion.58
  716.3 8.3 fusion.58
  740.2 8.3 fusion.58
  764.1 8.3 fusion.58
  773.3 11.5 all-gather
  785.2 9.8 all-gather.1
  796.2 8.6 while.36
  809.6 13.6 psum.99
  823.3 92.4 %fusion.27 = f32[16,512,8,1]{1,2,0,3:T(8,128)} fusion(bf16[32,512,16,512]{1,3,2,0:T(8,128)(2,1)} %get-tuple-element.181, f32[32,16,512]{2,0,1:T(8,128)} %copy.32, f32[8,32,512]{2,0,1:T(8,128)S(1)} %bitcast.140), kind=kOutput, calls=%fused_computation.47 | convolution fusion | flops 2151677952 | bytes 270270464 | tf_op jit(solution)/shard_map/bijr,irjc->bjc/dot_general | solution.py:112
  919.2 39.6 %psum.100 = f32[8]{0:T(128)S(1)} all-reduce(f32[8]{0:T(128)S(1)} %get-tuple-element.259), channel_id=1, replica_groups=mesh['src'=4,'dst'=8] {'src','dst'}, use_global_device_ids=true, to_apply=%region_11.12 | all-reduce | flops 8 | bytes 64 | tf_op jit(solution)/shard_map/psum | solution.py:122
  960.6 27.8 %all-gather.7.cloned.1.call-done = f32[8,65536]{1,0:T(8,128)} async-done(((f32[8,8192]{1,0:T(8,128)}), f32[8,65536]{1,0:T(8,128)}) %all-gather.7.cloned.1.call-update) | async-done | bytes 2097168 | tf_op jit(solution)/shard_map/all_gather | solution.py:90
  989.4 92.4 %fusion.25 = f32[16,512,8,1]{1,2,0,3:T(8,128)} fusion(bf16[32,512,16,512]{1,3,2,0:T(8,128)(2,1)} %get-tuple-element.181, f32[8,32,512]{2,0,1:T(8,128)S(1)} %bitcast.138, f32[32,16,512]{2,0,1:T(8,128)} %copy.32), kind=kOutput, calls=%fused_computation.45 | convolution fusion | flops 2151677952 | bytes 270270464 | tf_op jit(solution)/shard_map/bijr,irjc->bjc/dot_general | solution.py:112
  1083.7 39.4 %psum.102 = f32[8]{0:T(128)S(1)} all-reduce(f32[8]{0:T(128)S(1)} %multiply_reduce_fusion.1), channel_id=1, replica_groups=mesh['src'=4,'dst'=8] {'src','dst'}, use_global_device_ids=true, to_apply=%region_14.15 | all-reduce | flops 8 | bytes 64 | tf_op jit(solution)/shard_map/psum | solution.py:122
  1125.0 28.5 %all-gather.9.cloned.1.call-done = f32[8,65536]{1,0:T(8,128)} async-done(((f32[8,8192]{1,0:T(8,128)}), f32[8,65536]{1,0:T(8,128)}) %all-gather.9.cloned.1.call-update) | async-done | bytes 2097168 | tf_op jit(solution)/shard_map/all_gather | solution.py:90
  1154.6 85.0 %fusion.16 = (f32[8,32,16]{0,1,2:T(8,128)}, f32[8]{0:T(128)S(1)}, f32[8,32,512]{2,0,1:T(8,128)}, bf16[8,32,16,512]{3,0,1,2:T(8,128)(2,1)}) fusion(f32[32,16,512]{2,0,1:T(8,128)} %copy.32, f32[8,32,512]{2,0,1:T(8,128)S(1)} %bitcast.143, bf16[8,16,512,1]{2,0,3,1:T(8,128)(2,1)S(1)} %bitcast.162, bf16[32,512,16,512]{1,3,2,0:T(8,128)(2,1)} %get-tuple-element.181), kind=kOutput, calls=%fused_computation.33 | convolution fusion | flops 2164125696 | bytes 274874400 | tf_op jit(solution)/shard_map/irjc,bjc->bijr/dot_general | solution.py:131
  1239.7 39.4 %psum.106 = f32[8]{0:T(128)S(1)} all-reduce(f32[8]{0:T(128)S(1)} %get-tuple-element.218), channel_id=1, replica_groups=mesh['src'=4,'dst'=8] {'src','dst'}, use_global_device_ids=true, to_apply=%region_21.22 | all-reduce | flops 8 | bytes 64 | tf_op jit(solution)/shard_map/psum | solution.py:139
  1279.0 15.6 all-reduce.14.cloned.1.call-done
  1296.7 45.1 %all-gather.11.cloned.1.call-done = f32[8,65536]{1,0:T(8,128)} async-done(((f32[8,16384]{1,0:T(8,128)}), f32[8,65536]{1,0:T(8,128)}) %all-gather.11.cloned.1.call-update) | async-done | bytes 2097168 | tf_op jit(solution)/shard_map/all_gather | solution.py:98
  1342.8 84.0 %fusion.15 = (f32[8,32,16]{0,1,2:T(8,128)}, f32[8]{0:T(128)S(1)}, f32[8,32,512]{2,0,1:T(8,128)}) fusion(f32[32,16,512]{2,0,1:T(8,128)} %copy.32, f32[8,32,512]{2,0,1:T(8,128)S(1)} %bitcast.139, bf16[8,16,512,1]{2,0,3,1:T(8,128)(2,1)S(1)} %bitcast.163, bf16[32,512,16,512]{1,3,2,0:T(8,128)(2,1)} %get-tuple-element.181), kind=kOutput, calls=%fused_computation.30 | convolution fusion | flops 2164125696 | bytes 270680096 | tf_op jit(solution)/shard_map/irjc,bjc->bijr/dot_general | solution.py:131
  1426.9 39.3 %psum.108 = f32[8]{0:T(128)S(1)} all-reduce(f32[8]{0:T(128)S(1)} %get-tuple-element.215), channel_id=1, replica_groups=mesh['src'=4,'dst'=8] {'src','dst'}, use_global_device_ids=true, to_apply=%region_25.26 | all-reduce | flops 8 | bytes 64 | tf_op jit(solution)/shard_map/psum | solution.py:139
  1466.2 14.5 all-reduce.16.cloned.1.call-done
  1482.8 93.0 %fusion.23 = f32[16,512,8,1]{1,2,0,3:T(8,128)} fusion(bf16[32,512,16,512]{1,3,2,0:T(8,128)(2,1)} %get-tuple-element.181, bf16[8,32,16,512]{3,0,1,2:T(8,128)(2,1)} %get-tuple-element.255), kind=kOutput, calls=%fused_computation.43 | convolution fusion | flops 2147483648 | bytes 272891904 | tf_op jit(solution)/shard_map/bijr,irjc->bjc/dot_general | solution.py:112
  1579.8 83.6 %fusion.14 = (f32[8,32,16]{0,1,2:T(8,128)}, f32[8]{0:T(128)S(1)}, f32[8,32,512]{2,0,1:T(8,128)}) fusion(f32[32,16,512]{2,0,1:T(8,128)} %copy.32, f32[8,32,512]{2,0,1:T(8,128)S(1)} %bitcast.141, bf16[8,16,512,1]{2,0,3,1:T(8,128)(2,1)} %bitcast.164, bf16[32,512,16,512]{1,3,2,0:T(8,128)(2,1)} %get-tuple-element.181), kind=kOutput, calls=%fused_computation.27 | convolution fusion | flops 2164125696 | bytes 270680096 | tf_op jit(solution)/shard_map/irjc,bjc->bijr/dot_general | solution.py:131
  1664.6 39.3 %all-reduce = (f32[8]{0:T(128)S(1)}, f32[8]{0:T(128)S(1)}, f32[3,8]{1,0:T(4,128)S(1)}) all-reduce(f32[8]{0:T(128)S(1)} %get-tuple-element.257, f32[8]{0:T(128)S(1)} %get-tuple-element.212, f32[3,8]{1,0:T(4,128)S(1)} %fusion.30), channel_id=1, replica_groups=mesh['src'=4,'dst'=8] {'src','dst'}, use_global_device_ids=true, to_apply=%region_17.18 | all-reduce | flops 40 | bytes 320 | tf_op jit(solution)/shard_map/psum | solution.py:122
  1704.6 14.1 all-reduce.18.cloned.1.call-done
  1720.7 35.0 %all-reduce.12.cloned.1.call-done = f32[8,8192]{1,0:T(8,128)} async-done(((f32[8,8192]{1,0:T(8,128)}), f32[8,8192]{1,0:T(8,128)}) %all-reduce.12.cloned.1.call-update) | async-done | bytes 262160 | tf_op jit(solution)/shard_map/psum | solution.py:86
  (408 shorter events, 489.8 us)
Async XLA Ops:
  7.2 908.5 %copy-start = (bf16[8192,128]{1,0:T(8,128)(2,1)S(1)}, bf16[8192,128]{1,0:T(8,128)(2,1)}, u32[]{:S(2)}) copy-start(bf16[8192,128]{1,0:T(8,128)(2,1)} %param.15) | copy-start | bytes 6291460
  8.1 788.0 %copy-start.7 = (s32[32,16]{0,1:T(8,128)S(1)}, s32[32,16]{0,1:T(8,128)}, u32[]{:S(2)}) copy-start(s32[32,16]{0,1:T(8,128)} %param.18) | copy-start | bytes 6148
  12.2 5.7 copy-start.1
  36.1 5.7 copy-start.1
  60.1 5.7 copy-start.1
  84.0 5.7 copy-start.1
  108.0 5.7 copy-start.1
  131.9 5.7 copy-start.1
  155.8 5.7 copy-start.1
  179.7 5.7 copy-start.1
  203.6 5.7 copy-start.1
  227.5 5.7 copy-start.1
  251.4 5.7 copy-start.1
  275.3 5.7 copy-start.1
  299.1 5.7 copy-start.1
  323.1 5.7 copy-start.1
  346.9 5.7 copy-start.1
  370.8 5.7 copy-start.1
  394.7 5.7 copy-start.1
  418.7 5.7 copy-start.1
  442.6 5.7 copy-start.1
  466.5 5.7 copy-start.1
  490.5 5.7 copy-start.1
  514.4 5.7 copy-start.1
  538.3 5.7 copy-start.1
  562.2 5.7 copy-start.1
  586.1 5.7 copy-start.1
  610.0 5.7 copy-start.1
  633.9 5.7 copy-start.1
  657.8 5.7 copy-start.1
  681.7 5.7 copy-start.1
  705.6 5.7 copy-start.1
  729.5 5.7 copy-start.1
  753.4 5.7 copy-start.1
  773.3 34.7 %copy-start.8 = (s32[3,8]{1,0:T(4,128)S(1)}, s32[3,8]{1,0:T(4,128)}, u32[]{:S(2)}) copy-start(s32[3,8]{1,0:T(4,128)} %param.19) | copy-start | bytes 292
  773.3 50.0 %copy-start.2 = (f32[8,16384]{1,0:T(8,128)S(1)}, f32[8,16384]{1,0:T(8,128)}, u32[]{:S(2)}) copy-start(f32[8,16384]{1,0:T(8,128)} %param.20) | copy-start | bytes 1572868
  823.3 92.4 %copy-start.6 = (f32[8192]{0:T(1024)S(1)}, f32[8192]{0:T(1024)}, u32[]{:S(2)}) copy-start(f32[8192]{0:T(1024)} %param.17) | copy-start | bytes 98308
  916.9 206.2 %copy-start.4 = (f32[24,8192]{1,0:T(8,128)}, f32[24,8192]{1,0:T(8,128)S(1)}, u32[]{:S(2)}) copy-start(f32[24,8192]{1,0:T(8,128)S(1)} %fusion.13) | copy-start | bytes 2359300
  918.4 40.3 %all-reduce.8.cloned.1.call-start = ((), (), s32[]{:S(2)}) async-start(), calls=%async_computation | async-start | bytes 524288 | tf_op jit(solution)/shard_map/psum | solution.py:86
  919.2 69.2 %all-gather.7.cloned.1.call-start = ((), (), s32[]{:S(2)}) async-start(), calls=%async_computation.1 | async-start | bytes 2359296 | tf_op jit(solution)/shard_map/all_gather | solution.py:90
  1082.9 40.2 %all-reduce.10.cloned.1.call-start = ((), (), s32[]{:S(2)}) async-start(), calls=%async_computation.2 | async-start | bytes 524288 | tf_op jit(solution)/shard_map/psum | solution.py:86
  1083.7 69.8 %all-gather.9.cloned.1.call-start = ((), (), s32[]{:S(2)}) async-start(), calls=%async_computation.3 | async-start | bytes 2359296 | tf_op jit(solution)/shard_map/all_gather | solution.py:90
  1124.9 169.8 %all-reduce.14.cloned.1.call-start = ((), (), s32[]{:S(2)}) async-start(), calls=%async_computation.5 | async-start | bytes 1048576 | tf_op jit(solution)/shard_map/psum | solution.py:95
  1239.6 102.1 %all-gather.11.cloned.1.call-start = ((), (), s32[]{:S(2)}) async-start(), calls=%async_computation.6 | async-start | bytes 2621440 | tf_op jit(solution)/shard_map/all_gather | solution.py:98
  1296.6 184.1 %all-reduce.16.cloned.1.call-start = ((), (), s32[]{:S(2)}) async-start(), calls=%async_computation.7 | async-start | bytes 1048576 | tf_op jit(solution)/shard_map/psum | solution.py:95
  1426.9 151.1 %all-gather.13.cloned.1.call-start = ((), (), s32[]{:S(2)}) async-start(), calls=%async_computation.8 | async-start | bytes 2621440 | tf_op jit(solution)/shard_map/all_gather | solution.py:98
  1482.7 236.1 %all-reduce.18.cloned.1.call-start = ((), (), s32[]{:S(2)}) async-start(), calls=%async_computation.9 | async-start | bytes 1048576 | tf_op jit(solution)/shard_map/psum | solution.py:95
  1482.7 95.2 %copy-start.5 = (f32[24,8192]{1,0:T(8,128)S(1)}, f32[24,8192]{1,0:T(8,128)}, u32[]{:S(2)}) copy-start(f32[24,8192]{1,0:T(8,128)} %copy-done.4) | copy-start | bytes 2359300
  1482.7 97.0 %copy-start.3 = (f32[8,16384]{1,0:T(8,128)S(1)}, f32[8,16384]{1,0:T(8,128)}, u32[]{:S(2)}) copy-start(f32[8,16384]{1,0:T(8,128)} %param.20) | copy-start | bytes 1572868
  1664.4 91.2 %all-reduce.12.cloned.1.call-start = ((), (), s32[]{:S(2)}) async-start(), calls=%async_computation.4 | async-start | bytes 524288 | tf_op jit(solution)/shard_map/psum | solution.py:86
Sparse Core Ops, SparseCore 0:
  922.1 35.2 all-reduce.7
  960.7 27.6 all-gather.6
  1086.6 35.8 all-reduce.9
  1125.0 28.4 all-gather.8
  1239.8 54.8 all-reduce.13
  1296.8 44.9 all-gather.10
  1427.0 53.7 all-reduce.15
  1482.9 44.9 all-gather.12
  1664.6 54.1 all-reduce.17
  1720.9 34.7 all-reduce.11
where the time goes:
time: 1770 us; the launch traced here: 1760 us
  matrix products  662 us (37%)
  other arithmetic  450 us (25%)
  blocking collectives  232 us (13%)
  local copies, waits for them, and re-layouts  223 us (13%)
  waiting for transfers between devices  182 us (10%)
    dot_general x3, matrix products, local(): jnp.einsum('bijr,irjc->bjc', mix_terms, transit, preferred_element_type=j...  278 us
    reduce_sum x32, other arithmetic, table_block(): block_sum = jnp.sum(jnp.exp(scores - block_top[:, :, None]), axis=2)  265 us
    dot_general x3, matrix products, local(): jnp.einsum('irjc,bjc->bijr', transit, weights, preferred_element_type=jnp...  253 us
    while x64, local copies, waits for them, and re-layouts  182 us
    dynamic_update_slice x32, other arithmetic, local(): lax.scan(table_block, 0, (src_emb.reshape(row_blocks, BLK, emb_width), bl...  159 us
    dot_general x32, matrix products, table_block(): lax.dot_general(src_rows, dst_emb, (((1,), (1,)), ((), ())), preferred_el...  129 us
    psum x3, blocking collectives, local(): forward_total = lax.psum(forward_scale, ('src', 'dst'))  118 us
    psum x2, blocking collectives, local(): backward_total = lax.psum(backward_scale, ('src', 'dst'))  78.7 us
  transfers between devices with their start and end apart: 10, of which 7 were waited for; matrix products, arithmetic and copies ran while one was open for 6% of the time, Pallas kernels for 0%

commit v1 on v0

v1 whole, which is shorter than its diff:
```python
import functools

import jax
import jax.numpy as jnp
from jax import lax
from jax.experimental import pallas as pl
from jax.experimental.pallas import tpu as pltpu
from jax.sharding import PartitionSpec as P

BLK = 512
STEPS = 3
NB = 128
LANES = 128
DEPTH = 8
very_negative = -1e30
VMEM_BYTES = 60 * 1024 * 1024


def table_kernel(unit, cols, ids, count, src, dst, top, mass, transit, buf, sems):
    number = count[0]
    chunk = min(256, unit)

    def copy(slot, b):
        return pltpu.make_async_copy(buf.at[b], transit.at[slot], sems.at[b])

    def body(slot, carry):
        b = lax.rem(slot, 2)
        entry = ids[slot]
        i = lax.div(entry, cols)
        j = lax.rem(entry, cols)

        @pl.when(slot >= 2)
        def _():
            copy(slot - 2, b).wait()

        d = dst[pl.ds(pl.multiple_of(j * BLK, BLK), BLK), :]
        for c in range(unit // chunk):
            base = pl.multiple_of(i * unit + c * chunk, chunk)
            scores = lax.dot_general(
                d, src[pl.ds(base, chunk), :], (((1,), (1,)), ((), ())),
                preferred_element_type=jnp.float32,
            )
            best = jnp.max(scores, axis=0, keepdims=True)
            risen = jnp.exp(scores - best)
            buf[b, :, c * chunk:(c + 1) * chunk] = risen.astype(jnp.bfloat16)
            top[pl.ds(j, 1), pl.ds(base, chunk)] = best
            mass[pl.ds(j, 1), pl.ds(base, chunk)] = jnp.sum(risen, axis=0, keepdims=True)
        copy(slot, b).start()
        return carry

    lax.fori_loop(0, number, body, 0)
    for back in (2, 1):

        @pl.when(number >= back)
        def _():
            copy(number - back, lax.rem(number - back, 2)).wait()


def sweep_kernel(unit, cols, traces, kind, ids, count, *refs):
    if kind == 2:
        alpha, early, factor, weight, transit, pred, carried, terms, buf, sems = refs
    elif kind == 1:
        alpha, factor, weight, transit, pred, carried, terms, buf, sems = refs
    else:
        alpha, factor, weight, transit, pred, carried, buf, sems = refs
    number = count[0]
    pred[...] = jnp.zeros_like(pred)
    carried[...] = jnp.zeros_like(carried)
    if kind:
        terms[...] = jnp.zeros_like(terms)

    def copy(slot, b):
        return pltpu.make_async_copy(transit.at[slot], buf.at[b], sems.at[b])

    for p in range(DEPTH):

        @pl.when(p < number)
        def _():
            copy(p, p).start()

    def body(slot, carry):
        b = lax.rem(slot, DEPTH)
        entry = ids[slot]
        i = lax.div(entry, cols)
        j = lax.rem(entry, cols)
        rows = pl.ds(pl.multiple_of(i * unit, unit), unit)
        places = pl.ds(pl.multiple_of(j * BLK, BLK), BLK)
        share = factor[pl.ds(j, 1), rows]
        mix = (alpha[:, rows] * share).astype(jnp.bfloat16)
        w = weight[:, places].astype(jnp.bfloat16)
        copy(slot, b).wait()
        pred[:, places] += lax.dot_general(
            mix, buf[b], (((1,), (1,)), ((), ())), preferred_element_type=jnp.float32
        )
        spread = jnp.dot(w, buf[b], preferred_element_type=jnp.float32)
        carried[:, rows] += share * spread[:traces]

        @pl.when(slot + DEPTH < number)
        def _():
            copy(slot + DEPTH, b).start()

        if kind:
            group = pl.ds(pl.multiple_of(lax.div(entry, LANES) * LANES, LANES), LANES)
            hit = lax.broadcasted_iota(jnp.int32, (traces, LANES), 1) == lax.rem(entry, LANES)

            def note(t, m, s):
                value = jnp.sum(m.astype(jnp.float32) * s, axis=1, keepdims=True)
                terms[t, :, group] += jnp.where(hit, value, 0.0)

            if kind == 1:
                note(0, mix, spread)
            else:
                first = (early[:, rows] * share).astype(jnp.bfloat16)
                note(0, first, spread[:traces])
                note(1, mix, spread[traces:])
        return carry

    lax.fori_loop(0, number, body, 0)


def local(
    src_emb, dst_emb, out_emb, word_table, log_norm, block_mask, tokens, alpha_start, beta_end
):
    row_count, emb_width = src_emb.shape
    col_count = dst_emb.shape[0]
    traces = alpha_start.shape[0]
    src_count = lax.axis_size("src")
    dst_count = lax.axis_size("dst")
    states = row_count * src_count
    group = dst_count // src_count
    piece = col_count // src_count
    unit = min(BLK, piece)
    units = row_count // unit
    cols = col_count // BLK
    places = units * cols
    padded = -(-places // LANES) * LANES
    src_place = lax.axis_index("src")
    dst_place = lax.axis_index("dst")
    both = ("src", "dst")
    moves = [
        ((d // group) * dst_count + (d % group) * src_count + z, z * dst_count + d)
        for z in range(src_count)
        for d in range(dst_count)
    ]

    def spread_rows(mine):
        moved = lax.ppermute(mine, both, moves)
        return lax.all_gather(moved, "dst", axis=0, tiled=True)

    mine = lax.dynamic_slice_in_dim(src_emb, dst_place * piece, piece, 0)
    src_rows = spread_rows(mine)
    alpha_piece = lax.dynamic_slice_in_dim(alpha_start, dst_place * piece, piece, 1)
    alpha_moved = lax.ppermute(alpha_piece, both, moves)
    alpha_rows = lax.all_gather(alpha_moved, "dst", axis=1, tiled=True)

    whole_mask = lax.all_gather(block_mask, "src", axis=0, tiled=True)
    unit_index = jnp.arange(units, dtype=jnp.int32)
    per_piece = piece // unit
    unit_state = (
        (unit_index // per_piece) * col_count + src_place * piece + (unit_index % per_piece) * unit
    )
    unit_block = unit_state // BLK
    owner = unit_block[:, None] == jnp.arange(whole_mask.shape[0], dtype=jnp.int32)[None, :]
    mask = jnp.sum(jnp.where(owner[:, :, None], whole_mask[None], 0), axis=1)
    flat = (mask == 1).reshape(places)
    index = jnp.arange(places, dtype=jnp.int32)
    before = jnp.sum(
        jnp.where((index[None, :] < index[:, None]) & flat[None, :], 1, 0), axis=1
    )
    ids = jnp.sum(
        jnp.where((before[None, :] == index[:, None]) & flat[None, :], index[None, :], 0), axis=1
    ).astype(jnp.int32)
    number = jnp.sum(flat.astype(jnp.int32)).reshape(1)

    smem = pl.BlockSpec(memory_space=pltpu.SMEM)
    vmem = pl.BlockSpec(memory_space=pltpu.VMEM)
    anywhere = pl.BlockSpec(memory_space=pl.ANY)
    guess = places // 5 + 1
    params = pltpu.CompilerParams(vmem_limit_bytes=VMEM_BYTES)
    top, mass, transit = pl.pallas_call(
        functools.partial(table_kernel, unit, cols),
        out_shape=(
            jax.ShapeDtypeStruct((cols, row_count), jnp.float32),
            jax.ShapeDtypeStruct((cols, row_count), jnp.float32),
            jax.ShapeDtypeStruct((places, BLK, unit), jnp.bfloat16),
        ),
        in_specs=[smem, smem, vmem, vmem],
        out_specs=(vmem, vmem, anywhere),
        scratch_shapes=[
            pltpu.VMEM((2, BLK, unit), jnp.bfloat16),
            pltpu.SemaphoreType.DMA((2,)),
        ],
        compiler_params=params,
        cost_estimate=pl.CostEstimate(
            flops=guess * BLK * unit * emb_width * 2,
            bytes_accessed=guess * BLK * unit * 2,
            transcendentals=guess * BLK * unit,
        ),
        name="table",
    )(ids, number, src_rows, dst_emb)

    vocab_slice = word_table.shape[0]
    local_ids = tokens.reshape(-1) - dst_place * vocab_slice
    onehot = (local_ids[:, None] == jnp.arange(vocab_slice, dtype=jnp.int32)[None, :]).astype(
        jnp.bfloat16
    )
    looked = jnp.dot(onehot, word_table, preferred_element_type=jnp.float32)
    word_rows = lax.psum(looked.astype(jnp.bfloat16), "dst")
    logits = lax.dot_general(
        word_rows, out_emb, (((1,), (1,)), ((), ())), preferred_element_type=jnp.float32
    )
    emission = jnp.exp(logits - log_norm[None, :]).reshape(STEPS, traces, col_count)
    emission_piece = lax.dynamic_slice_in_dim(emission, src_place * piece, piece, 2)

    allowed = jnp.repeat((mask == 1).T, unit, axis=1)
    row_best = jnp.max(jnp.where(allowed, top, very_negative), axis=0)
    row_mass = jnp.sum(jnp.where(allowed, mass * jnp.exp(top - row_best[None, :]), 0.0), axis=0)
    pairs = lax.all_gather(jnp.stack([row_best, row_mass]), "dst", axis=0)
    whole_best = jnp.max(pairs[:, 0], axis=0)
    whole_mass = jnp.sum(pairs[:, 1] * jnp.exp(pairs[:, 0] - whole_best[None]), axis=0)
    log_total = whole_best + jnp.log(whole_mass)
    factor = jnp.where(allowed, jnp.exp(top - log_total[None, :]), 0.0)

    def sweep(kind, alphas, weights):
        outs = [
            jax.ShapeDtypeStruct((traces, col_count), jnp.float32),
            jax.ShapeDtypeStruct((traces, row_count), jnp.float32),
        ]
        if kind:
            outs.append(jax.ShapeDtypeStruct((kind, traces, padded), jnp.float32))
        return pl.pallas_call(
            functools.partial(sweep_kernel, unit, cols, traces, kind),
            out_shape=tuple(outs),
            in_specs=[smem, smem] + [vmem] * (len(alphas) + 2) + [anywhere],
            out_specs=(vmem,) * len(outs),
            scratch_shapes=[
                pltpu.VMEM((DEPTH, BLK, unit), jnp.bfloat16),
                pltpu.SemaphoreType.DMA((DEPTH,)),
            ],
            compiler_params=params,
            cost_estimate=pl.CostEstimate(
                flops=guess * BLK * unit * traces * 4,
                bytes_accessed=guess * BLK * unit * 2,
                transcendentals=0,
            ),
            name="sweep%d" % kind,
        )(ids, number, *alphas, factor, weights, transit)

    def tail(value):
        return jnp.broadcast_to(value[:, None, None], (traces, 1, LANES))

    def exchange_forward(partial_value, position):
        scale = jnp.sum(partial_value * emission[position], axis=1)
        payload = jnp.concatenate(
            [
                partial_value.reshape(traces, src_count, piece),
                jnp.broadcast_to(tail(scale), (traces, src_count, LANES)),
            ],
            axis=2,
        )
        part = lax.psum_scatter(payload, "src", scatter_dimension=1, tiled=False)
        part = jnp.concatenate(
            [part[:, :piece] * emission_piece[position], part[:, piece:]], axis=1
        )
        gathered = lax.all_gather(part, "dst", axis=1)
        total = jnp.sum(gathered[:, :, piece], axis=1) / states
        return gathered[:, :, :piece].reshape(traces, row_count) / total[:, None]

    def exchange_backward(partial_value):
        scale = jnp.sum(partial_value, axis=1)
        payload = jnp.concatenate(
            [
                partial_value.reshape(traces, dst_count, piece),
                jnp.broadcast_to(tail(scale), (traces, dst_count, LANES)),
            ],
            axis=2,
        )
        part = lax.psum_scatter(payload, "dst", scatter_dimension=1, tiled=False)
        gathered = lax.all_gather(part, "src", axis=1)
        total = jnp.sum(gathered[:, :, piece], axis=1) / states
        return gathered[:, :, :piece].reshape(traces, col_count) / total[:, None]

    last_weights = emission[2] * beta_end
    pred, carried = sweep(0, [alpha_rows], last_weights)
    alpha_1 = exchange_forward(pred, 0)
    weights_2 = emission[1] * exchange_backward(carried)
    pred, carried, middle_terms = sweep(1, [alpha_1], weights_2)
    alpha_2 = exchange_forward(pred, 1)
    weights_1 = emission[0] * exchange_backward(carried)
    pred, carried, end_terms = sweep(
        2, [alpha_2, alpha_rows], jnp.concatenate([weights_1, last_weights], axis=0)
    )

    block_terms = jnp.concatenate([middle_terms, end_terms], axis=0)[:, :, :places]
    scales = jnp.concatenate(
        [
            jnp.sum(pred * emission[2], axis=1)[None],
            jnp.sum(carried, axis=1)[None],
            jnp.sum(block_terms, axis=2),
        ],
        axis=0,
    )
    totals = lax.psum(scales, both)
    predicted = lax.psum(pred, "src")
    alpha_end = predicted * emission[2] / (totals[0] / states)[:, None]

    part = lax.psum_scatter(
        carried.reshape(traces, dst_count, piece), "dst", scatter_dimension=1, tiled=False
    )
    back = lax.ppermute(part, both, [(b, a) for a, b in moves])
    gathered = lax.all_gather(back, "dst", axis=1, tiled=True)
    beta_start = gathered / (totals[1] / states)[:, None]

    counts = jnp.sum(block_terms / totals[2:][:, :, None], axis=(0, 1)) * (
        NB * NB / (STEPS * traces)
    )
    counts = counts.reshape(units, cols)
    placed = jnp.sum(jnp.where(owner[:, :, None], counts[:, None, :], 0.0), axis=0)
    block_counts = lax.psum_scatter(placed, "src", scatter_dimension=0, tiled=True)
    return (alpha_end, beta_start, block_counts)


def solution(mesh):
    return jax.shard_map(
        local,
        mesh=mesh,
        in_specs=(
            P("src", None),
            P("dst", None),
            P("dst", None),
            P("dst", None),
            P("dst"),
            P("src", "dst"),
            P(),
            P(None, "src"),
            P(None, "dst"),
        ),
        out_specs=(P(None, "dst"), P(None, "src"), P("src", "dst")),
        check_vma=False,
    )
```

time: 1770 us -> 642 us (0.36)
  matrix products: 662 us -> 2.74 us
  other arithmetic: 450 us -> 33 us
  local copies, waits for them, and re-layouts: 223 us -> 8.35 us
  Pallas kernels: 0 us -> 166 us
  blocking collectives: 232 us -> 184 us
  waiting for transfers between devices: 182 us -> 229 us
    dot_general x38 -> x0, matrix products: 659 us -> none  [the longest x3 278 us: local(): jnp.einsum('bijr,irjc->bjc', mix_terms, transit, preferred_element_type=j...]
    reduce_sum x67 -> x17, other arithmetic: 269 us -> 10.6 us  [the longest x2 2.67 us: exchange_backward(): scale = jnp.sum(partial_value, axis=1)]
    while x65 -> x0, local copies, waits for them, and re-layouts: 183 us -> none
    pallas_call x0 -> x4, Pallas kernels: none -> 166 us  [the longest x3 107 us: sweep(): pl.pallas_call(functools.partial(sweep_kernel, unit, cols, traces, kind),...]
    dynamic_update_slice x32 -> x0, other arithmetic: 159 us -> none  [local(): lax.scan(table_block, 0, (src_emb.reshape(row_blocks, BLK, emb_width), bl...]
    psum x5 -> x1, blocking collectives: 197 us -> 45.9 us  [local(): totals = lax.psum(scales, both)]
    unnamed x10 -> x14, waiting for transfers between devices: 1.5 us -> 140 us
    all_gather x2 -> x7, blocking collectives: 21.3 us -> 125 us  [the longest x1 46.1 us: local(): whole_mask = lax.all_gather(block_mask, 'src', axis=0, tiled=True)]
  transfers between devices with their start and end apart: 10 -> 12, of which waited for: 7 -> 8; matrix products, arithmetic and copies ran while one was open for 6% -> 3% of each run, Pallas kernels for 0% -> 9%
where the time goes in v1:
time: 642 us; the launch traced here: 640 us
  waiting for transfers between devices  229 us (36%)
  blocking collectives  184 us (29%)
  Pallas kernels  166 us (26%)
  other arithmetic  33 us (5%)
  between operations  14.2 us (2%)
  local copies, waits for them, and re-layouts  8.35 us (1%)
    unnamed x14, waiting for transfers between devices  140 us
    pallas_call x3, Pallas kernels, sweep(): pl.pallas_call(functools.partial(sweep_kernel, unit, cols, traces, kind),...  107 us
    pallas_call x1, Pallas kernels, local(): pl.pallas_call(functools.partial(table_kernel, unit, cols), out_shape=(ja...  59.1 us
    all_gather x1, blocking collectives, local(): whole_mask = lax.all_gather(block_mask, 'src', axis=0, tiled=True)  46.1 us
    psum x1, blocking collectives, local(): totals = lax.psum(scales, both)  45.9 us
    psum x1, waiting for transfers between devices, local(): predicted = lax.psum(pred, 'src')  37.1 us
    reduce_scatter x1, waiting for transfers between devices, local(): lax.psum_scatter(carried.reshape(traces, dst_count, piece), 'dst', scatte...  34 us
    all_gather x2, blocking collectives, exchange_backward(): gathered = lax.all_gather(part, 'src', axis=1)  28.5 us
  transfers between devices with their start and end apart: 12, of which 8 were waited for; matrix products, arithmetic and copies ran while one was open for 3% of the time, Pallas kernels for 9%

profile of v1, /device:TPU:0, one launch (start us, length us, event | category | flops | bytes accessed | tf_op | source)
XLA Modules:
  0.0 639.9 jit_solution(2511391519481836921)
XLA Ops:
  7.3 1.2 constant_dynamic-slice_fusion
  8.5 0.7 collective-permute-start.1
  9.2 0.8 copy-done.6
  10.1 0.9 constant_dynamic-slice_fusion.1
  10.9 0.7 collective-permute-start
  11.6 46.1 %all-gather.3 = s32[4,32,16]{1,2,0:T(8,128)S(1)} all-gather(s32[1,32,16]{1,2,0:T(8,128)} %bitcast.84), channel_id=1, replica_groups=mesh['src'=4,'dst'=8] {'src'}, dimensions={0}, use_global_device_ids=true | all-gather | bytes 10240 | tf_op jit(solution)/shard_map/all_gather | solution.py:156
  57.9 0.6 select_reduce_fusion.5
  58.5 0.7 convert_reduce_fusion
  59.6 0.2 copy.28
  59.9 1.5 convolution_convert_fusion
  61.4 13.2 %psum.21 = bf16[24,128]{1,0:T(8,128)(2,1)S(1)} all-reduce(bf16[24,128]{1,0:T(8,128)(2,1)S(1)} %convolution_convert_fusion), channel_id=1, replica_groups=mesh['src'=4,'dst'=8] {'dst'}, use_global_device_ids=true, to_apply=%region_8.9 | all-reduce | flops 3072 | bytes 12288 | tf_op jit(solution)/shard_map/psum | solution.py:208
  74.8 0.9 select_reduce_fusion.2.ids
  75.7 1.2 fusion
  76.9 59.1 %table.1 = (f32[16,16384]{1,0:T(8,128)}, f32[16,16384]{1,0:T(8,128)}, bf16[512,512,512]{2,1,0:T(8,128)(2,1)}) custom-call(s32[512]{0:T(512)} %select_reduce_fusion.2.ids, s32[1]{0:T(128)} %bitcast.1.count, bf16[16384,128]{1,0:T(8,128)(2,1)} %all-gather.8.cloned.1.call-done.src, bf16[8192,128]{1,0:T(8,128)(2,1)} %dst.1), custom_call_target="tpu_custom_call" | custom-call | flops 6912212992 | bytes 54001664 | tf_op jit(solution)/shard_map/table/pallas_call | solution.py:180
  136.1 1.6 select_reduce_fusion.1
  137.7 1.6 select_reduce_fusion
  139.3 0.8 maximum_bitcast_fusion
  140.2 0.7 slice_multiply_fusion.refs_2_
  140.9 20.5 %all_gather.37.refs_0_.refs_1_ = f32[8,16384]{1,0:T(8,128)} all-gather(f32[8,2048]{1,0:T(8,128)S(1)} %collective-permute-done), channel_id=1, replica_groups=mesh['src'=4,'dst'=8] {'dst'}, dimensions={1}, use_global_device_ids=true | all-gather | bytes 589824 | tf_op jit(solution)/shard_map/all_gather | solution.py:154
  161.4 17.5 %all-gather.10.cloned.1.call-done = f32[8,2,16384]{2,1,0:T(2,128)} async-done(((f32[1,2,16384]{2,1,0:T(2,128)}), f32[8,2,16384]{2,1,0:T(2,128)}) %all-gather.10.cloned.1.call-update) | async-done | bytes 1048592 | tf_op jit(solution)/shard_map/all_gather | solution.py:218
  178.8 2.9 fusion.13
  181.7 0.8 fusion.4
  182.5 1.2 exponential_select_fusion.refs_1_.refs_2_
  183.7 31.0 %sweep0.1 = (f32[8,8192]{1,0:T(8,128)}, f32[8,16384]{1,0:T(8,128)}) custom-call(s32[512]{0:T(512)} %select_reduce_fusion.2.ids, s32[1]{0:T(128)} %bitcast.1.count, f32[8,16384]{1,0:T(8,128)} %all_gather.37.refs_0_.refs_1_, f32[16,16384]{1,0:T(8,128)} %exponential_select_fusion.refs_1_.refs_2_, f32[8,8192]{1,0:T(8,128)} %slice_multiply_fusion.refs_2_, ...), custom_call_target="tpu_custom_call" | custom-call | flops 864026624 | bytes 54001664 | tf_op jit(solution)/shard_map/sweep0/pallas_call | solution.py:231
  214.8 1.3 reduce_sum.179
  216.2 1.9 pad_maximum_fusion
  218.2 40.7 %reduce-scatter.23.cloned.1.call-done = f32[8,1,2176]{2,0,1:T(8,128)} async-done(((f32[8,8,2176]{2,0,1:T(8,128)}), f32[8,1,2176]{2,0,1:T(8,128)}) %reduce-scatter.23.cloned.1.call-update) | async-done | bytes 69648
  258.9 14.2 %all_gather.43 = f32[8,4,2176]{2,0,1:T(8,128)S(1)} all-gather(f32[8,1,2176]{2,0,1:T(8,128)} %reduce-scatter.23.cloned.1.call-done), channel_id=1, replica_groups=mesh['src'=4,'dst'=8] {'src'}, dimensions={1}, use_global_device_ids=true | all-gather | bytes 348160 | tf_op jit(solution)/shard_map/all_gather | solution.py:279
  273.3 0.9 divide_multiply_fusion.1
  274.3 0.7 pad_maximum_fusion.3
  275.1 20.7 %reduce-scatter.21.cloned.1.call-done = f32[8,1,2176]{2,0,1:T(8,128)} async-done(((f32[8,4,2176]{2,0,1:T(8,128)}), f32[8,1,2176]{2,0,1:T(8,128)}) %reduce-scatter.21.cloned.1.call-update) | async-done | bytes 69648
  295.8 0.7 slice.101
  296.4 0.8 fusion.8
  297.3 10.0 %all-gather.1 = f32[8,17408]{1,0:T(8,128)S(1)} all-gather(f32[8,2176]{1,0:T(8,128)S(1)} %pad_maximum_fusion.5), channel_id=3, replica_groups=mesh['src'=4,'dst'=8] {'dst'}, dimensions={1}, use_global_device_ids=true | all-gather | bytes 626688 | tf_op jit(solution)/shard_map/all_gather | solution.py:265
  307.4 0.9 broadcast_divide_fusion.2.refs_0_
  308.3 37.6 %sweep1.1 = (f32[8,8192]{1,0:T(8,128)}, f32[8,16384]{1,0:T(8,128)}, f32[1,8,512]{2,1,0:T(8,128)}) custom-call(s32[512]{0:T(512)} %select_reduce_fusion.2.ids, s32[1]{0:T(128)} %bitcast.1.count, f32[8,16384]{1,0:T(8,128)} %broadcast_divide_fusion.2.refs_0_, f32[16,16384]{1,0:T(8,128)} %exponential_select_fusion.refs_1_.refs_2_, ...), custom_call_target="tpu_custom_call" | custom-call | flops 864026624 | bytes 54001664 | tf_op jit(solution)/shard_map/sweep1/pallas_call | solution.py:231
  345.9 1.3 reduce_sum.183
  347.3 1.9 pad_maximum_fusion.1
  349.3 39.6 %reduce-scatter.27.cloned.1.call-done = f32[8,1,2176]{2,0,1:T(8,128)} async-done(((f32[8,8,2176]{2,0,1:T(8,128)}), f32[8,1,2176]{2,0,1:T(8,128)}) %reduce-scatter.27.cloned.1.call-update) | async-done | bytes 69648
  388.9 14.3 %all_gather.46 = f32[8,4,2176]{2,0,1:T(8,128)S(1)} all-gather(f32[8,1,2176]{2,0,1:T(8,128)} %reduce-scatter.27.cloned.1.call-done), channel_id=1, replica_groups=mesh['src'=4,'dst'=8] {'src'}, dimensions={1}, use_global_device_ids=true | all-gather | bytes 348160 | tf_op jit(solution)/shard_map/all_gather | solution.py:279
  403.3 0.9 divide_multiply_fusion
  404.3 0.7 pad_maximum_fusion.4
  405.2 1.8 pad_maximum_fusion.2.refs_3_
  406.9 18.9 %reduce-scatter.25.cloned.1.call-done = f32[8,1,2176]{2,0,1:T(8,128)} async-done(((f32[8,4,2176]{2,0,1:T(8,128)}), f32[8,1,2176]{2,0,1:T(8,128)}) %reduce-scatter.25.cloned.1.call-update) | async-done | bytes 69648
  425.8 0.7 slice.108
  426.5 0.8 fusion.7
  427.3 9.9 %all-gather.2 = f32[8,17408]{1,0:T(8,128)S(1)} all-gather(f32[8,2176]{1,0:T(8,128)S(1)} %pad_maximum_fusion.6), channel_id=4, replica_groups=mesh['src'=4,'dst'=8] {'dst'}, dimensions={1}, use_global_device_ids=true | all-gather | bytes 626688 | tf_op jit(solution)/shard_map/all_gather | solution.py:265
  437.4 0.9 broadcast_divide_fusion.1.refs_0_
  438.4 38.0 %sweep2.1 = (f32[8,8192]{1,0:T(8,128)}, f32[8,16384]{1,0:T(8,128)}, f32[2,8,512]{2,1,0:T(8,128)}) custom-call(s32[512]{0:T(512)} %select_reduce_fusion.2.ids, s32[1]{0:T(128)} %bitcast.1.count, f32[8,16384]{1,0:T(8,128)} %broadcast_divide_fusion.1.refs_0_, f32[8,16384]{1,0:T(8,128)} %all_gather.37.refs_0_.refs_1_, ...), custom_call_target="tpu_custom_call" | custom-call | flops 864026624 | bytes 54001664 | tf_op jit(solution)/shard_map/sweep2/pallas_call | solution.py:231
  476.4 0.8 constant_dynamic-update-slice_fusion
  477.3 1.1 multiply_reduce_fusion
  478.4 1.3 reduce_sum.186
  479.7 45.9 %psum.23 = f32[5,8]{1,0:T(8,128)S(1)} all-reduce(f32[5,8]{1,0:T(8,128)S(1)} %pad_maximum_fusion.7), channel_id=1, replica_groups=mesh['src'=4,'dst'=8] {'src','dst'}, use_global_device_ids=true, to_apply=%region_25.26 | all-reduce | flops 40 | bytes 320 | tf_op jit(solution)/shard_map/psum | solution.py:303
  525.9 0.7 copy.24
  526.7 0.7 reduce-scatter.17.cloned.1.call-update
  527.4 0.7 all-reduce.6.cloned.1.call-update
  528.1 18.8 %reduce-scatter.19.cloned.1.call-done = f32[32,16]{1,0:T(8,128)} async-done(((f32[128,16]{1,0:T(8,128)}), f32[32,16]{1,0:T(8,128)}) %reduce-scatter.19.cloned.1.call-update) | async-done | bytes 2064
  546.9 1.4 copy.25
  548.3 34.0 %reduce-scatter.17.cloned.1.call-done = f32[8,1,2048]{2,0,1:T(8,128)} async-done(((f32[8,8,2048]{2,0,1:T(8,128)}), f32[8,1,2048]{2,0,1:T(8,128)}) %reduce-scatter.17.cloned.1.call-update) | async-done | bytes 65552 | tf_op jit(solution)/shard_map/reduce_scatter | solution.py:307
  582.4 1.5 collective-permute-start.2
  583.8 37.1 %all-reduce.6.cloned.1.call-done = f32[8,8192]{1,0:T(8,128)} async-done(((f32[8,8192]{1,0:T(8,128)}), f32[8,8192]{1,0:T(8,128)}) %all-reduce.6.cloned.1.call-update) | async-done | bytes 262160 | tf_op jit(solution)/shard_map/psum | solution.py:304
  620.9 1.7 multiply_divide_fusion
  622.6 9.8 %all_gather.47 = f32[8,16384]{1,0:T(8,128)S(1)} all-gather(f32[8,2048]{1,0:T(8,128)S(1)} %collective-permute-done.2), channel_id=1, replica_groups=mesh['src'=4,'dst'=8] {'dst'}, dimensions={1}, use_global_device_ids=true | all-gather | bytes 589824 | tf_op jit(solution)/shard_map/all_gather | solution.py:311
  632.4 0.9 broadcast_divide_fusion
  (83 shorter events, 2.7 us)
Async XLA Ops:
  7.2 68.5 %copy-start = (bf16[8192,128]{1,0:T(8,128)(2,1)S(1)}, bf16[8192,128]{1,0:T(8,128)(2,1)}, u32[]{:S(2)}) copy-start(bf16[8192,128]{1,0:T(8,128)(2,1)} %param.11) | copy-start | bytes 6291460
  7.2 52.6 %copy-start.12 = (s32[3,8]{1,0:T(4,128)S(1)}, s32[3,8]{1,0:T(4,128)}, u32[]{:S(2)}) copy-start(s32[3,8]{1,0:T(4,128)} %param.15) | copy-start | bytes 292
  7.2 68.5 %copy-start.10 = (f32[8192]{0:T(1024)S(1)}, f32[8192]{0:T(1024)}, u32[]{:S(2)}) copy-start(f32[8192]{0:T(1024)} %param.13) | copy-start | bytes 98308
  7.2 69.7 %all-gather.8.cloned.1.call-start = ((), (), s32[]{:S(2)}) async-start(), calls=%async_computation.6 | async-start | bytes 4718592 | tf_op jit(solution)/shard_map/all_gather | solution.py:148
  8.5 0.7 collective-permute-start.1
  9.2 0.8 copy-start.6
  10.0 168.8 %all-gather.10.cloned.1.call-start = ((), (), s32[]{:S(2)}) async-start(), calls=%async_computation.9 | async-start | bytes 1179648 | tf_op jit(solution)/shard_map/all_gather | solution.py:218
  10.9 130.0 %collective-permute-start = (f32[8,2048]{1,0:T(8,128)S(1)}, f32[8,2048]{1,0:T(8,128)S(1)}, u32[]{:S(2)}, u32[]{:S(2)}) collective-permute-start(f32[8,2048]{1,0:T(8,128)S(1)} %constant_dynamic-slice_fusion.1), channel_id=1, source_target_pairs={{0,0},{4,1},{8,2},{12,3},{16,4},{20,5},{24,6},{28,7},{1,8},{5,9},{... | collective-permute-start | bytes 196616 | tf_op jit(solution)/shard_map/ppermute | solution.py:153
  57.9 1.4 copy-start.8
  136.1 1.6 copy-start.1
  136.1 4.1 copy-start.7
  140.1 118.8 %reduce-scatter.23.cloned.1.call-start = ((), (), s32[]{:S(2)}) async-start(), calls=%async_computation.12 | async-start | bytes 626688
  178.8 3.7 copy-start.2
  214.8 58.5 %copy-start.5 = (f32[8,8192]{1,0:T(8,128)S(1)}, f32[8,8192]{1,0:T(8,128)}, u32[]{:S(2)}) copy-start(f32[8,8192]{1,0:T(8,128)} %get-tuple-element.17) | copy-start | bytes 786436
  218.1 77.6 %reduce-scatter.21.cloned.1.call-start = ((), (), s32[]{:S(2)}) async-start(), calls=%async_computation.11 | async-start | bytes 348160
  275.0 113.9 %reduce-scatter.27.cloned.1.call-start = ((), (), s32[]{:S(2)}) async-start(), calls=%async_computation.14 | async-start | bytes 626688
  345.9 3.4 copy-start.11
  345.9 57.4 %copy-start.4 = (f32[8,8192]{1,0:T(8,128)S(1)}, f32[8,8192]{1,0:T(8,128)}, u32[]{:S(2)}) copy-start(f32[8,8192]{1,0:T(8,128)} %get-tuple-element.19) | copy-start | bytes 786436
  349.2 55.9 %copy-start.3 = (f32[8,8192]{1,0:T(8,128)S(1)}, f32[8,8192]{1,0:T(8,128)}, u32[]{:S(2)}) copy-start(f32[8,8192]{1,0:T(8,128)} %slice_multiply_fusion.refs_2_) | copy-start | bytes 786436
  349.3 76.5 %reduce-scatter.25.cloned.1.call-start = ((), (), s32[]{:S(2)}) async-start(), calls=%async_computation.13 | async-start | bytes 348160
  405.1 141.8 %reduce-scatter.19.cloned.1.call-start = ((), (), s32[]{:S(2)}) async-start(), calls=%async_computation.10 | async-start | bytes 81920
  438.4 87.4 %copy-start.9 = (pred[32,128]{1,0:T(8,128)(4,1)S(1)}, pred[32,128]{1,0:T(8,128)(4,1)}, u32[]{:S(2)}) copy-start(pred[32,128]{1,0:T(8,128)(4,1)} %copy-done.8) | copy-start | bytes 12292
  526.6 55.7 %reduce-scatter.17.cloned.1.call-start = ((), (), s32[]{:S(2)}) async-start(), calls=%async_computation.8 | async-start | bytes 589824 | tf_op jit(solution)/shard_map/reduce_scatter | solution.py:307
  527.4 93.5 %all-reduce.6.cloned.1.call-start = ((), (), s32[]{:S(2)}) async-start(), calls=%async_computation.7 | async-start | bytes 524288 | tf_op jit(solution)/shard_map/psum | solution.py:304
  582.4 40.3 %collective-permute-start.2 = (f32[8,2048]{1,0:T(8,128)}, f32[8,2048]{1,0:T(8,128)S(1)}, u32[]{:S(2)}, u32[]{:S(2)}) collective-permute-start(f32[8,2048]{1,0:T(8,128)} %bitcast.87), channel_id=1, source_target_pairs={{0,0},{1,4},{2,8},{3,12},{4,16},{5,20},{6,24},{7,28},{8,1},{9,5},{... | collective-permute-start | bytes 196616 | tf_op jit(solution)/shard_map/ppermute | solution.py:310
Sparse Core Ops, SparseCore 0:
  10.5 66.2 all-gather.7
  140.2 38.5 all-gather.9
  218.3 40.5 reduce-scatter.22
  275.1 20.5 reduce-scatter.20
  349.4 39.5 reduce-scatter.26
  405.2 20.5 reduce-scatter.24
  526.8 20.1 reduce-scatter.18
  550.0 32.2 reduce-scatter.16
  585.3 35.5 all-reduce.5

commit v2 on v1

--- a/solution.py
+++ b/solution.py
@@ -116,6 +116,79 @@
         return carry
 
     lax.fori_loop(0, number, body, 0)
+
+
+def exchange_kernel(
+    lines, piece, states, ahead, behind, glow, alpha, beta,
+    in_f, in_b, red_f, red_b, land_f, land_b, send_1, recv_1, send_2, recv_2,
+):
+    place = {name: lax.axis_index(name) for name in lines}
+    mesh_ids = pl.DeviceIdType.MESH
+
+    def peer(name, k):
+        return lax.rem(place[name] + k, lines[name])
+
+    def origin(name, k):
+        return lax.rem(place[name] + lines[name] - k, lines[name])
+
+    barrier = pltpu.get_barrier_semaphore()
+    for name in lines:
+        for k in range(1, lines[name]):
+            pl.semaphore_signal(
+                barrier, inc=1, device_id={name: peer(name, k)}, device_id_type=mesh_ids
+            )
+    pl.semaphore_wait(barrier, sum(lines.values()) - len(lines))
+
+    offset = {"src": 0, "dst": lines["src"]}
+    payload = {"src": ahead, "dst": behind}
+    landing = {"src": in_f, "dst": in_b}
+    first = {"src": [], "dst": []}
+    for name in lines:
+        for k in range(1, lines[name]):
+            copy = pltpu.make_async_remote_copy(
+                src_ref=payload[name].at[peer(name, k)],
+                dst_ref=landing[name].at[k],
+                send_sem=send_1.at[offset[name] + k],
+                recv_sem=recv_1.at[offset[name] + k],
+                device_id={name: peer(name, k)},
+                device_id_type=mesh_ids,
+            )
+            copy.start()
+            first[name].append(copy)
+    second = []
+    for name, other, red, land in (("src", "dst", red_f, land_f), ("dst", "src", red_b, land_b)):
+        value = payload[name][place[name]]
+        for k in range(1, lines[name]):
+            first[name][k - 1].wait_recv()
+            value = value + landing[name][k]
+        if name == "src":
+            value = jnp.concatenate([value[:, :piece] * glow[...], value[:, piece:]], axis=1)
+        red[...] = value
+        for k in range(1, lines[other]):
+            copy = pltpu.make_async_remote_copy(
+                src_ref=red,
+                dst_ref=land.at[k],
+                send_sem=send_2.at[offset[other] + k],
+                recv_sem=recv_2.at[offset[other] + k],
+                device_id={other: peer(other, k)},
+                device_id_type=mesh_ids,
+            )
+            copy.start()
+            second.append(copy)
+    for copy in second:
+        copy.wait_recv()
+    for other, red, land, out in (("dst", red_f, land_f, alpha), ("src", red_b, land_b, beta)):
+        total = red[:, piece:piece + 1]
+        for k in range(1, lines[other]):
+            total = total + land[k, :, piece:piece + 1]
+        scale = total / states
+        for k in range(lines[other]):
+            part = red[:, :piece] if k == 0 else land[k, :, :piece]
+            start = pl.multiple_of(origin(other, k) * piece, piece)
+            out[:, pl.ds(start, piece)] = part / scale
+    for copies in (first["src"], first["dst"], second):
+        for copy in copies:
+            copy.wait_send()
 
 
 def local(
@@ -246,47 +319,54 @@
             name="sweep%d" % kind,
         )(ids, number, *alphas, factor, weights, transit)
 
-    def tail(value):
-        return jnp.broadcast_to(value[:, None, None], (traces, 1, LANES))
-
-    def exchange_forward(partial_value, position):
-        scale = jnp.sum(partial_value * emission[position], axis=1)
-        payload = jnp.concatenate(
-            [
-                partial_value.reshape(traces, src_count, piece),
-                jnp.broadcast_to(tail(scale), (traces, src_count, LANES)),
-            ],
-            axis=2,
+    def exchange(ahead, behind, position):
+        def payload(value, scale, number):
+            return jnp.concatenate(
+                [
+                    value.reshape(traces, number, piece).transpose(1, 0, 2),
+                    jnp.broadcast_to(scale[None, :, None], (number, traces, LANES)),
+                ],
+                axis=2,
+            )
+
+        width = piece + LANES
+        semaphores = pltpu.SemaphoreType.DMA((src_count + dst_count,))
+        return pl.pallas_call(
+            functools.partial(
+                exchange_kernel, {"src": src_count, "dst": dst_count}, piece, states
+            ),
+            out_shape=(
+                jax.ShapeDtypeStruct((traces, row_count), jnp.float32),
+                jax.ShapeDtypeStruct((traces, col_count), jnp.float32),
+            ),
+            in_specs=[vmem] * 3,
+            out_specs=(vmem, vmem),
+            scratch_shapes=[
+                pltpu.VMEM((src_count, traces, width), jnp.float32),
+                pltpu.VMEM((dst_count, traces, width), jnp.float32),
+                pltpu.VMEM((traces, width), jnp.float32),
+                pltpu.VMEM((traces, width), jnp.float32),
+                pltpu.VMEM((dst_count, traces, width), jnp.float32),
+                pltpu.VMEM((src_count, traces, width), jnp.float32),
+            ]
+            + [semaphores] * 4,
+            compiler_params=pltpu.CompilerParams(
+                collective_id=0, has_side_effects=True, vmem_limit_bytes=VMEM_BYTES
+            ),
+            name="exchange",
+        )(
+            payload(ahead, jnp.sum(ahead * emission[position], axis=1), src_count),
+            payload(behind, jnp.sum(behind, axis=1), dst_count),
+            emission_piece[position],
         )
-        part = lax.psum_scatter(payload, "src", scatter_dimension=1, tiled=False)
-        part = jnp.concatenate(
-            [part[:, :piece] * emission_piece[position], part[:, piece:]], axis=1
-        )
-        gathered = lax.all_gather(part, "dst", axis=1)
-        total = jnp.sum(gathered[:, :, piece], axis=1) / states
-        return gathered[:, :, :piece].reshape(traces, row_count) / total[:, None]
-
-    def exchange_backward(partial_value):
-        scale = jnp.sum(partial_value, axis=1)
-        payload = jnp.concatenate(
-            [
-                partial_value.reshape(traces, dst_count, piece),
-                jnp.broadcast_to(tail(scale), (traces, dst_count, LANES)),
-            ],
-            axis=2,
-        )
-        part = lax.psum_scatter(payload, "dst", scatter_dimension=1, tiled=False)
-        gathered = lax.all_gather(part, "src", axis=1)
-        total = jnp.sum(gathered[:, :, piece], axis=1) / states
-        return gathered[:, :, :piece].reshape(traces, col_count) / total[:, None]
 
     last_weights = emission[2] * beta_end
     pred, carried = sweep(0, [alpha_rows], last_weights)
-    alpha_1 = exchange_forward(pred, 0)
-    weights_2 = emission[1] * exchange_backward(carried)
+    alpha_1, beta_2 = exchange(pred, carried, 0)
+    weights_2 = emission[1] * beta_2
     pred, carried, middle_terms = sweep(1, [alpha_1], weights_2)
-    alpha_2 = exchange_forward(pred, 1)
-    weights_1 = emission[0] * exchange_backward(carried)
+    alpha_2, beta_1 = exchange(pred, carried, 1)
+    weights_1 = emission[0] * beta_1
     pred, carried, end_terms = sweep(
         2, [alpha_2, alpha_rows], jnp.concatenate([weights_1, last_weights], axis=0)
     )
@@ -300,13 +380,12 @@
         ],
         axis=0,
     )
-    totals = lax.psum(scales, both)
-    predicted = lax.psum(pred, "src")
+    totals = jnp.sum(lax.all_gather(scales, both, axis=0), axis=0)
+    predicted = jnp.sum(lax.all_gather(pred, "src", axis=0), axis=0)
     alpha_end = predicted * emission[2] / (totals[0] / states)[:, None]
 
-    part = lax.psum_scatter(
-        carried.reshape(traces, dst_count, piece), "dst", scatter_dimension=1, tiled=False
-    )
+    parts = carried.reshape(traces, dst_count, piece).transpose(1, 0, 2)
+    part = jnp.sum(lax.all_to_all(parts, "dst", 0, 0, tiled=False), axis=0)
     back = lax.ppermute(part, both, [(b, a) for a, b in moves])
     gathered = lax.all_gather(back, "dst", axis=1, tiled=True)
     beta_start = gathered / (totals[1] / states)[:, None]
@@ -316,7 +395,9 @@
     )
     counts = counts.reshape(units, cols)
     placed = jnp.sum(jnp.where(owner[:, :, None], counts[:, None, :], 0.0), axis=0)
-    block_counts = lax.psum_scatter(placed, "src", scatter_dimension=0, tiled=True)
+    mask_rows = block_mask.shape[0]
+    everyone = jnp.sum(lax.all_gather(placed, "src", axis=0), axis=0)
+    block_counts = lax.dynamic_slice_in_dim(everyone, src_place * mask_rows, mask_rows, 0)
     return (alpha_end, beta_start, block_counts)
 
 

time: 642 us -> 453 us (0.71)
  waiting for transfers between devices: 229 us -> 9.26 us
  Pallas kernels: 166 us -> 208 us
  blocking collectives: 184 us -> 170 us
    unnamed x14 -> x3, waiting for transfers between devices: 140 us -> 0.05 us
    pallas_call x0 -> x2, Pallas kernels: none -> 56 us  [exchange(): pl.pallas_call(functools.partial(exchange_kernel, {'src': src_count, 'dst...]
    psum x1 -> x0, blocking collectives: 45.9 us -> none  [local(): totals = lax.psum(scales, both)]
    psum x1 -> x0, waiting for transfers between devices: 37.1 us -> none  [local(): predicted = lax.psum(pred, 'src')]
    reduce_scatter x1 -> x0, waiting for transfers between devices: 34 us -> none  [local(): lax.psum_scatter(carried.reshape(traces, dst_count, piece), 'dst', scatte...]
    all_gather x4 -> x2, blocking collectives: 48.4 us -> 64 us  [the longest x1 50.8 us: local(): totals = jnp.sum(lax.all_gather(scales, both, axis=0), axis=0)]
    all_gather x1, blocking collectives: 20.5 us -> 30 us  [local(): alpha_rows = lax.all_gather(alpha_moved, 'dst', axis=1, tiled=True)]
    pallas_call x3, Pallas kernels: 107 us -> 97.6 us  [sweep(): pl.pallas_call(functools.partial(sweep_kernel, unit, cols, traces, kind),...]
  transfers between devices with their start and end apart: 12 -> 7, of which waited for: 8 -> 1; matrix products, arithmetic and copies ran while one was open for 3% -> 4% of each run, Pallas kernels for 9% -> 12%
where the time goes in v2:
time: 453 us; the launch traced here: 448 us
  Pallas kernels  208 us (46%)
  blocking collectives  170 us (38%)
  other arithmetic  31.6 us (7%)
  between operations  14.1 us (3%)
  waiting for transfers between devices  9.26 us (2%)
  local copies, waits for them, and re-layouts  6.13 us (1%)
  starting transfers between devices  5.63 us (1%)
    pallas_call x3, Pallas kernels, sweep(): pl.pallas_call(functools.partial(sweep_kernel, unit, cols, traces, kind),...  97.6 us
    pallas_call x2, Pallas kernels, exchange(): pl.pallas_call(functools.partial(exchange_kernel, {'src': src_count, 'dst...  56 us
    pallas_call x1, Pallas kernels, local(): pl.pallas_call(functools.partial(table_kernel, unit, cols), out_shape=(ja...  54 us
    all_gather x1, blocking collectives, local(): totals = jnp.sum(lax.all_gather(scales, both, axis=0), axis=0)  50.8 us
    all_gather x1, blocking collectives, local(): whole_mask = lax.all_gather(block_mask, 'src', axis=0, tiled=True)  46.1 us
    all_gather x1, blocking collectives, local(): alpha_rows = lax.all_gather(alpha_moved, 'dst', axis=1, tiled=True)  30 us
    all_gather x1, blocking collectives, local(): gathered = lax.all_gather(back, 'dst', axis=1, tiled=True)  17.2 us
    psum x1, blocking collectives, local(): word_rows = lax.psum(looked.astype(jnp.bfloat16), 'dst')  13.2 us
  transfers between devices with their start and end apart: 7, of which 1 were waited for; matrix products, arithmetic and copies ran while one was open for 4% of the time, Pallas kernels for 12%

profile of v2, /device:TPU:0, one launch (start us, length us, event | category | flops | bytes accessed | tf_op | source)
XLA Modules:
  0.0 447.5 jit_solution(559516810252728405)
XLA Ops:
  7.3 1.2 constant_dynamic-slice_fusion.1
  8.5 0.7 collective-permute-start.1
  9.2 0.8 copy-done.6
  10.1 0.9 constant_dynamic-slice_fusion.2
  10.9 0.7 collective-permute-start
  11.6 46.1 %all-gather.4 = s32[4,32,16]{1,2,0:T(8,128)S(1)} all-gather(s32[1,32,16]{1,2,0:T(8,128)} %bitcast.71), channel_id=1, replica_groups=mesh['src'=4,'dst'=8] {'src'}, dimensions={0}, use_global_device_ids=true | all-gather | bytes 10240 | tf_op jit(solution)/shard_map/all_gather | solution.py:229
  57.7 0.1 reshape.162
  57.8 0.1 iota_compare_fusion.4
  57.9 0.6 select_reduce_fusion.5
  58.5 0.7 convert_reduce_fusion
  59.2 0.1 eq.64
  59.3 0.1 copy.22
  59.4 0.1 broadcast_in_dim.119
  59.6 0.2 copy.29
  59.8 0.1 sub.65
  59.9 1.5 convolution_convert_fusion
  61.4 13.2 %psum.7 = bf16[24,128]{1,0:T(8,128)(2,1)S(1)} all-reduce(bf16[24,128]{1,0:T(8,128)(2,1)S(1)} %convolution_convert_fusion), channel_id=1, replica_groups=mesh['src'=4,'dst'=8] {'dst'}, use_global_device_ids=true, to_apply=%region_8.9 | all-reduce | flops 3072 | bytes 12288 | tf_op jit(solution)/shard_map/psum | solution.py:281
  74.6 0.2 select_reduce_fusion.3
  74.8 0.9 select_reduce_fusion.2.ids
  75.7 1.2 fusion
  76.9 54.0 %table.1 = (f32[16,16384]{1,0:T(8,128)}, f32[16,16384]{1,0:T(8,128)}, bf16[512,512,512]{2,1,0:T(8,128)(2,1)}) custom-call(s32[512]{0:T(512)} %select_reduce_fusion.2.ids, s32[1]{0:T(128)} %bitcast.1.count, bf16[16384,128]{1,0:T(8,128)(2,1)} %all-gather.11.cloned.1.call-done.src, bf16[8192,128]{1,0:T(8,128)(2,1)} %dst.1), custom_call_target="tpu_custom_call" | custom-call | flops 6912212992 | bytes 54001664 | tf_op jit(solution)/shard_map/table/pallas_call | solution.py:253
  130.9 1.6 select_reduce_fusion.1
  132.5 1.6 select_reduce_fusion
  134.2 0.8 maximum_bitcast_fusion
  135.0 0.7 slice_multiply_fusion.2.refs_2_
  135.8 0.7 dynamic-slice_bitcast_fusion
  136.4 30.0 %all_gather.37.refs_0_.refs_1_ = f32[8,16384]{1,0:T(8,128)} all-gather(f32[8,2048]{1,0:T(8,128)S(1)} %collective-permute-done), channel_id=1, replica_groups=mesh['src'=4,'dst'=8] {'dst'}, dimensions={1}, use_global_device_ids=true | all-gather | bytes 589824 | tf_op jit(solution)/shard_map/all_gather | solution.py:227
  166.4 9.2 %all-gather.15.cloned.1.call-done = f32[8,2,16384]{2,1,0:T(2,128)} async-done(((f32[1,2,16384]{2,1,0:T(2,128)}), f32[8,2,16384]{2,1,0:T(2,128)}) %all-gather.15.cloned.1.call-update) | async-done | bytes 1048592 | tf_op jit(solution)/shard_map/all_gather | solution.py:291
  175.6 2.9 fusion.11
  178.5 0.8 fusion.4
  179.3 1.2 exponential_select_fusion.refs_1_.refs_2_
  180.5 28.4 %sweep0.1 = (f32[8,8192]{1,0:T(8,128)}, f32[8,16384]{1,0:T(8,128)}) custom-call(s32[512]{0:T(512)} %select_reduce_fusion.2.ids, s32[1]{0:T(128)} %bitcast.1.count, f32[8,16384]{1,0:T(8,128)} %all_gather.37.refs_0_.refs_1_, f32[16,16384]{1,0:T(8,128)} %exponential_select_fusion.refs_1_.refs_2_, f32[8,8192]{1,0:T(8,128)} %slice_multiply_fusion.2.refs_2_, ...), custom_call_target="tpu_custom_call" | custom-call | flops 864026624 | bytes 54001664 | tf_op jit(solution)/shard_map/sweep0/pallas_call | solution.py:304
  208.9 1.2 multiply_reduce_fusion.2
  210.1 1.3 reduce_sum.178
  211.4 0.1 broadcast_in_dim.123
  211.5 1.9 pad_maximum_fusion.behind
  213.5 0.7 pad_maximum_fusion.3.ahead
  214.2 26.7 %exchange.2 = (f32[8,16384]{1,0:T(8,128)}, f32[8,8192]{1,0:T(8,128)}) custom-call(f32[4,8,2176]{2,1,0:T(8,128)} %pad_maximum_fusion.3.ahead, f32[8,8,2176]{2,1,0:T(8,128)} %pad_maximum_fusion.behind, f32[8,2048]{1,0:T(8,128)} %get-tuple-element.39.glow), custom_call_target="tpu_custom_call" | custom-call | tf_op jit(solution)/shard_map/exchange/pallas_call | solution.py:334
  240.9 1.7 slice_multiply_fusion.refs_2_
  242.6 34.3 %sweep1.1 = (f32[8,8192]{1,0:T(8,128)}, f32[8,16384]{1,0:T(8,128)}, f32[1,8,512]{2,1,0:T(8,128)}) custom-call(s32[512]{0:T(512)} %select_reduce_fusion.2.ids, s32[1]{0:T(128)} %bitcast.1.count, f32[8,16384]{1,0:T(8,128)} %get-tuple-element.23.refs_0_, f32[16,16384]{1,0:T(8,128)} %exponential_select_fusion.refs_1_.refs_2_, ...), custom_call_target="tpu_custom_call" | custom-call | flops 864026624 | bytes 54001664 | tf_op jit(solution)/shard_map/sweep1/pallas_call | solution.py:304
  276.9 1.3 reduce_sum.180
  278.3 1.2 multiply_reduce_fusion.1
  279.5 1.9 pad_maximum_fusion.1.behind
  281.5 0.7 pad_maximum_fusion.4.ahead
  282.2 29.3 %exchange.3 = (f32[8,16384]{1,0:T(8,128)}, f32[8,8192]{1,0:T(8,128)}) custom-call(f32[4,8,2176]{2,1,0:T(8,128)} %pad_maximum_fusion.4.ahead, f32[8,8,2176]{2,1,0:T(8,128)} %pad_maximum_fusion.1.behind, f32[8,2048]{1,0:T(8,128)} %get-tuple-element.38.glow), custom_call_target="tpu_custom_call" | custom-call | tf_op jit(solution)/shard_map/exchange/pallas_call | solution.py:334
  311.5 1.0 slice_multiply_fusion.1
  312.5 0.8 pad_maximum_fusion.2.refs_3_
  313.4 34.8 %sweep2.1 = (f32[8,8192]{1,0:T(8,128)}, f32[8,16384]{1,0:T(8,128)}, f32[2,8,512]{2,1,0:T(8,128)}) custom-call(s32[512]{0:T(512)} %select_reduce_fusion.2.ids, s32[1]{0:T(128)} %bitcast.1.count, f32[8,16384]{1,0:T(8,128)} %get-tuple-element.27.refs_0_, f32[8,16384]{1,0:T(8,128)} %all_gather.37.refs_0_.refs_1_, ...), custom_call_target="tpu_custom_call" | custom-call | flops 864026624 | bytes 54001664 | tf_op jit(solution)/shard_map/sweep2/pallas_call | solution.py:304
  348.2 1.1 multiply_reduce_fusion
  349.4 0.8 constant_dynamic-update-slice_fusion
  350.1 0.1 reduce_sum.184
  350.2 1.3 reduce_sum.183
  351.5 50.8 %all-gather.6 = f32[32,5,8]{2,1,0:T(8,128)S(1)} all-gather(f32[1,5,8]{2,1,0:T(8,128)S(1)} %maximum_bitcast_fusion.1), channel_id=4, replica_groups=mesh['src'=4,'dst'=8] {'src','dst'}, dimensions={0}, use_global_device_ids=true | all-gather | bytes 5280 | tf_op jit(solution)/shard_map/all_gather | solution.py:383
  402.4 0.1 divide_reduce_fusion
  402.5 3.5 all-to-all-start
  406.0 0.1 mul.92
  406.1 0.1 select_reduce_fusion.4
  406.2 13.1 %all-gather.3 = f32[512,16]{0,1:T(8,128)S(1)} all-gather(f32[128,16]{0,1:T(8,128)S(1)} %select_reduce_fusion.4), channel_id=5, replica_groups=mesh['src'=4,'dst'=8] {'src'}, dimensions={0}, use_global_device_ids=true | all-gather | bytes 40960 | tf_op jit(solution)/shard_map/all_gather | solution.py:399
  419.5 0.7 collective-permute-start.2
  420.1 0.7 constant_dynamic-slice_fusion
  420.8 17.2 %all_gather.45 = f32[8,16384]{1,0:T(8,128)S(1)} all-gather(f32[8,2048]{1,0:T(8,128)S(1)} %collective-permute-done.2), channel_id=1, replica_groups=mesh['src'=4,'dst'=8] {'dst'}, dimensions={1}, use_global_device_ids=true | all-gather | bytes 589824 | tf_op jit(solution)/shard_map/all_gather | solution.py:390
  438.0 0.9 broadcast_divide_fusion
  438.9 1.3 bitcast_reduce_fusion
  440.2 0.8 multiply_divide_fusion
  (53 shorter events, 0.7 us)
Async XLA Ops:
  7.2 68.5 %copy-start = (bf16[8192,128]{1,0:T(8,128)(2,1)S(1)}, bf16[8192,128]{1,0:T(8,128)(2,1)}, u32[]{:S(2)}) copy-start(bf16[8192,128]{1,0:T(8,128)(2,1)} %param.11) | copy-start | bytes 6291460
  7.2 52.6 %copy-start.12 = (s32[3,8]{1,0:T(4,128)S(1)}, s32[3,8]{1,0:T(4,128)}, u32[]{:S(2)}) copy-start(s32[3,8]{1,0:T(4,128)} %param.15) | copy-start | bytes 292
  7.2 68.5 %copy-start.10 = (f32[8192]{0:T(1024)S(1)}, f32[8192]{0:T(1024)}, u32[]{:S(2)}) copy-start(f32[8192]{0:T(1024)} %param.13) | copy-start | bytes 98308
  7.2 69.7 %all-gather.11.cloned.1.call-start = ((), (), s32[]{:S(2)}) async-start(), calls=%async_computation.1 | async-start | bytes 4718592 | tf_op jit(solution)/shard_map/all_gather | solution.py:221
  8.5 0.7 collective-permute-start.1
  9.2 0.8 copy-start.6
  10.0 165.5 %all-gather.15.cloned.1.call-start = ((), (), s32[]{:S(2)}) async-start(), calls=%async_computation.3 | async-start | bytes 1179648 | tf_op jit(solution)/shard_map/all_gather | solution.py:291
  10.9 125.5 %collective-permute-start = (f32[8,2048]{1,0:T(8,128)S(1)}, f32[8,2048]{1,0:T(8,128)S(1)}, u32[]{:S(2)}, u32[]{:S(2)}) collective-permute-start(f32[8,2048]{1,0:T(8,128)S(1)} %constant_dynamic-slice_fusion.2), channel_id=1, source_target_pairs={{0,0},{4,1},{8,2},{12,3},{16,4},{20,5},{24,6},{28,7},{1,8},{5,9},{... | collective-permute-start | bytes 196616 | tf_op jit(solution)/shard_map/ppermute | solution.py:226
  57.9 1.4 copy-start.8
  130.9 1.6 copy-start.1
  130.9 4.1 copy-start.7
  135.0 303.9 %all-gather.13.cloned.1.call-start = ((), (), s32[]{:S(2)}) async-start(), calls=%async_computation.2 | async-start | bytes 1310720 | tf_op jit(solution)/shard_map/all_gather | solution.py:384
  175.6 3.7 copy-start.2
  208.9 4.5 %copy-start.5 = (f32[8,8192]{1,0:T(8,128)S(1)}, f32[8,8192]{1,0:T(8,128)}, u32[]{:S(2)}) copy-start(f32[8,8192]{1,0:T(8,128)} %get-tuple-element.21) | copy-start | bytes 786436
  276.9 4.6 %copy-start.4 = (f32[8,8192]{1,0:T(8,128)S(1)}, f32[8,8192]{1,0:T(8,128)}, u32[]{:S(2)}) copy-start(f32[8,8192]{1,0:T(8,128)} %get-tuple-element.25) | copy-start | bytes 786436
  278.3 34.3 %copy-start.3 = (f32[8,8192]{1,0:T(8,128)S(1)}, f32[8,8192]{1,0:T(8,128)}, u32[]{:S(2)}) copy-start(f32[8,8192]{1,0:T(8,128)} %slice_multiply_fusion.2.refs_2_) | copy-start | bytes 786436
  313.4 36.0 %copy-start.11 = (f32[1,8,512]{2,1,0:T(8,128)S(1)}, f32[1,8,512]{2,1,0:T(8,128)}, u32[]{:S(2)}) copy-start(f32[1,8,512]{2,1,0:T(8,128)} %get-tuple-element.31) | copy-start | bytes 49156
  348.2 57.9 %copy-start.9 = (pred[32,128]{1,0:T(8,128)(4,1)S(1)}, pred[32,128]{1,0:T(8,128)(4,1)}, u32[]{:S(2)}) copy-start(pred[32,128]{1,0:T(8,128)(4,1)} %copy-done.8) | copy-start | bytes 12292
  402.5 16.9 %all-to-all-start = ((f32[8,8,2048]{2,1,0:T(8,128)}), f32[8,8,2048]{2,1,0:T(8,128)S(1)}, u32[]{:S(2)}, u32[]{:S(2)}) async-start(f32[8,8,2048]{2,1,0:T(8,128)} %bitcast.62), calls=%async_computation | async-start | bytes 1048576 | tf_op jit(solution)/shard_map/all_to_all | solution.py:388
  419.5 1.4 collective-permute-start.2
Sparse Core Ops, SparseCore 0:
  10.5 66.2 all-gather.10
  135.1 40.4 all-gather.14
  349.5 39.2 all-gather.12

commit v3 on v2

--- a/solution.py
+++ b/solution.py
@@ -189,6 +189,46 @@
     for copies in (first["src"], first["dst"], second):
         for copy in copies:
             copy.wait_send()
+
+
+def total_kernel(lines, value, out, red, land_1, land_2, send_1, recv_1, send_2, recv_2):
+    place = {name: lax.axis_index(name) for name in lines}
+    mesh_ids = pl.DeviceIdType.MESH
+
+    def peer(name, k):
+        return lax.rem(place[name] + k, lines[name])
+
+    barrier = pltpu.get_barrier_semaphore()
+    for name in lines:
+        for k in range(1, lines[name]):
+            pl.semaphore_signal(
+                barrier, inc=1, device_id={name: peer(name, k)}, device_id_type=mesh_ids
+            )
+    pl.semaphore_wait(barrier, sum(lines.values()) - len(lines))
+
+    def line_sum(name, given, land, send, recv):
+        copies = []
+        for k in range(1, lines[name]):
+            copy = pltpu.make_async_remote_copy(
+                src_ref=given,
+                dst_ref=land.at[k],
+                send_sem=send.at[k],
+                recv_sem=recv.at[k],
+                device_id={name: peer(name, k)},
+                device_id_type=mesh_ids,
+            )
+            copy.start()
+            copies.append(copy)
+        total = given[...]
+        for k in range(1, lines[name]):
+            copies[k - 1].wait_recv()
+            total = total + land[k]
+        return total, copies
+
+    red[...], early = line_sum("src", value, land_1, send_1, recv_1)
+    out[...], late = line_sum("dst", red, land_2, send_2, recv_2)
+    for copy in early + late:
+        copy.wait_send()
 
 
 def local(
@@ -380,7 +420,23 @@
         ],
         axis=0,
     )
-    totals = jnp.sum(lax.all_gather(scales, both, axis=0), axis=0)
+    kinds = scales.shape[0]
+    shape = (-(-kinds // 8) * 8, -(-traces // LANES) * LANES)
+    totals = pl.pallas_call(
+        functools.partial(total_kernel, {"src": src_count, "dst": dst_count}),
+        out_shape=jax.ShapeDtypeStruct(shape, jnp.float32),
+        in_specs=[vmem],
+        out_specs=vmem,
+        scratch_shapes=[
+            pltpu.VMEM(shape, jnp.float32),
+            pltpu.VMEM((src_count,) + shape, jnp.float32),
+            pltpu.VMEM((dst_count,) + shape, jnp.float32),
+        ]
+        + [pltpu.SemaphoreType.DMA((src_count,))] * 2
+        + [pltpu.SemaphoreType.DMA((dst_count,))] * 2,
+        compiler_params=pltpu.CompilerParams(collective_id=1, has_side_effects=True),
+        name="totals",
+    )(jnp.pad(scales, ((0, shape[0] - kinds), (0, shape[1] - traces))))[:kinds, :traces]
     predicted = jnp.sum(lax.all_gather(pred, "src", axis=0), axis=0)
     alpha_end = predicted * emission[2] / (totals[0] / states)[:, None]
 

time: 453 us -> 423 us (0.934)
  blocking collectives: 170 us -> 106 us
  Pallas kernels: 208 us -> 236 us
    all_gather x1 -> x0, blocking collectives: 50.8 us -> none  [local(): totals = jnp.sum(lax.all_gather(scales, both, axis=0), axis=0)]
    pallas_call x3, Pallas kernels: 97.6 us -> 113 us  [sweep(): pl.pallas_call(functools.partial(sweep_kernel, unit, cols, traces, kind),...]
    pallas_call x0 -> x1, Pallas kernels: none -> 14.6 us  [local(): pl.pallas_call(functools.partial(total_kernel, {'src': src_count, 'dst':...]
    all_gather x1, blocking collectives: 30 us -> 16.4 us  [local(): alpha_rows = lax.all_gather(alpha_moved, 'dst', axis=1, tiled=True)]
    pallas_call x2, Pallas kernels: 56 us -> 45.4 us  [exchange(): pl.pallas_call(functools.partial(exchange_kernel, {'src': src_count, 'dst...]
    pallas_call x1, Pallas kernels: 54 us -> 63 us  [local(): pl.pallas_call(functools.partial(table_kernel, unit, cols), out_shape=(ja...]
  transfers between devices with their start and end apart: 7 -> 7, of which waited for: 1 -> 1; matrix products, arithmetic and copies ran while one was open for 4% -> 4% of each run, Pallas kernels for 12% -> 19%
where the time goes in v3:
time: 423 us; the launch traced here: 418 us
  Pallas kernels  236 us (56%)
  blocking collectives  106 us (25%)
  other arithmetic  33 us (8%)
  between operations  14.1 us (3%)
  waiting for transfers between devices  12.6 us (3%)
  local copies, waits for them, and re-layouts  6.81 us (2%)
  starting transfers between devices  5.77 us (1%)
    pallas_call x3, Pallas kernels, sweep(): pl.pallas_call(functools.partial(sweep_kernel, unit, cols, traces, kind),...  113 us
    pallas_call x1, Pallas kernels, local(): pl.pallas_call(functools.partial(table_kernel, unit, cols), out_shape=(ja...  63 us
    all_gather x1, blocking collectives, local(): whole_mask = lax.all_gather(block_mask, 'src', axis=0, tiled=True)  46.1 us
    pallas_call x2, Pallas kernels, exchange(): pl.pallas_call(functools.partial(exchange_kernel, {'src': src_count, 'dst...  45.4 us
    all_gather x1, blocking collectives, local(): gathered = lax.all_gather(back, 'dst', axis=1, tiled=True)  17.2 us
    all_gather x1, blocking collectives, local(): alpha_rows = lax.all_gather(alpha_moved, 'dst', axis=1, tiled=True)  16.4 us
    pallas_call x1, Pallas kernels, local(): pl.pallas_call(functools.partial(total_kernel, {'src': src_count, 'dst':...  14.6 us
    all_gather x1, blocking collectives, local(): everyone = jnp.sum(lax.all_gather(placed, 'src', axis=0), axis=0)  13.5 us
  transfers between devices with their start and end apart: 7, of which 1 were waited for; matrix products, arithmetic and copies ran while one was open for 4% of the time, Pallas kernels for 19%

profile of v3, /device:TPU:0, one launch (start us, length us, event | category | flops | bytes accessed | tf_op | source)
XLA Modules:
  0.0 417.8 jit_solution(16880135280930544139)
XLA Ops:
  7.3 1.2 constant_dynamic-slice_fusion.1
  8.5 0.7 collective-permute-start.1
  9.2 0.8 copy-done.6
  10.1 0.9 constant_dynamic-slice_fusion.2
  10.9 0.7 collective-permute-start
  11.6 46.1 %all-gather.3 = s32[4,32,16]{1,2,0:T(8,128)S(1)} all-gather(s32[1,32,16]{1,2,0:T(8,128)} %bitcast.69), channel_id=1, replica_groups=mesh['src'=4,'dst'=8] {'src'}, dimensions={0}, use_global_device_ids=true | all-gather | bytes 10240 | tf_op jit(solution)/shard_map/all_gather | solution.py:269
  57.7 0.1 reshape.161
  57.9 0.6 select_reduce_fusion.5
  58.5 0.7 convert_reduce_fusion
  59.2 0.1 eq.64
  59.3 0.1 copy.22
  59.4 0.1 broadcast_in_dim.119
  59.6 0.2 copy.29
  59.8 0.1 sub.65
  59.9 1.5 convolution_convert_fusion
  61.4 13.2 %psum.7 = bf16[24,128]{1,0:T(8,128)(2,1)S(1)} all-reduce(bf16[24,128]{1,0:T(8,128)(2,1)S(1)} %convolution_convert_fusion), channel_id=1, replica_groups=mesh['src'=4,'dst'=8] {'dst'}, use_global_device_ids=true, to_apply=%region_8.9 | all-reduce | flops 3072 | bytes 12288 | tf_op jit(solution)/shard_map/psum | solution.py:321
  74.6 0.2 select_reduce_fusion.3
  74.8 0.9 select_reduce_fusion.2.ids
  75.7 1.2 fusion
  76.9 63.0 %table.1 = (f32[16,16384]{1,0:T(8,128)}, f32[16,16384]{1,0:T(8,128)}, bf16[512,512,512]{2,1,0:T(8,128)(2,1)}) custom-call(s32[512]{0:T(512)} %select_reduce_fusion.2.ids, s32[1]{0:T(128)} %bitcast.1.count, bf16[16384,128]{1,0:T(8,128)(2,1)} %all-gather.9.cloned.1.call-done.src, bf16[8192,128]{1,0:T(8,128)(2,1)} %dst.1), custom_call_target="tpu_custom_call" | custom-call | flops 6912212992 | bytes 54001664 | tf_op jit(solution)/shard_map/table/pallas_call | solution.py:293
  139.9 1.6 select_reduce_fusion.1
  141.5 1.6 select_reduce_fusion
  143.2 0.8 maximum_bitcast_fusion
  144.0 0.7 slice_multiply_fusion.2.refs_2_
  144.8 0.7 dynamic-slice_bitcast_fusion
  145.4 16.4 %all_gather.31.refs_0_.refs_1_ = f32[8,16384]{1,0:T(8,128)} all-gather(f32[8,2048]{1,0:T(8,128)S(1)} %collective-permute-done), channel_id=1, replica_groups=mesh['src'=4,'dst'=8] {'dst'}, dimensions={1}, use_global_device_ids=true | all-gather | bytes 589824 | tf_op jit(solution)/shard_map/all_gather | solution.py:267
  161.8 12.5 %all-gather.13.cloned.1.call-done = f32[8,2,16384]{2,1,0:T(2,128)} async-done(((f32[1,2,16384]{2,1,0:T(2,128)}), f32[8,2,16384]{2,1,0:T(2,128)}) %all-gather.13.cloned.1.call-update) | async-done | bytes 1048592 | tf_op jit(solution)/shard_map/all_gather | solution.py:331
  174.3 2.9 fusion.11
  177.2 0.8 fusion.4
  178.0 1.2 exponential_select_fusion.refs_1_.refs_2_
  179.2 33.0 %sweep0.1 = (f32[8,8192]{1,0:T(8,128)}, f32[8,16384]{1,0:T(8,128)}) custom-call(s32[512]{0:T(512)} %select_reduce_fusion.2.ids, s32[1]{0:T(128)} %bitcast.1.count, f32[8,16384]{1,0:T(8,128)} %all_gather.31.refs_0_.refs_1_, f32[16,16384]{1,0:T(8,128)} %exponential_select_fusion.refs_1_.refs_2_, f32[8,8192]{1,0:T(8,128)} %slice_multiply_fusion.2.refs_2_, ...), custom_call_target="tpu_custom_call" | custom-call | flops 864026624 | bytes 54001664 | tf_op jit(solution)/shard_map/sweep0/pallas_call | solution.py:344
  212.2 1.2 multiply_reduce_fusion.2
  213.4 1.3 reduce_sum.169
  214.8 1.9 pad_maximum_fusion.behind
  216.7 0.7 pad_maximum_fusion.3.ahead
  217.4 22.7 %exchange.2 = (f32[8,16384]{1,0:T(8,128)}, f32[8,8192]{1,0:T(8,128)}) custom-call(f32[4,8,2176]{2,1,0:T(8,128)} %pad_maximum_fusion.3.ahead, f32[8,8,2176]{2,1,0:T(8,128)} %pad_maximum_fusion.behind, f32[8,2048]{1,0:T(8,128)} %get-tuple-element.39.glow), custom_call_target="tpu_custom_call" | custom-call | tf_op jit(solution)/shard_map/exchange/pallas_call | solution.py:374
  240.2 1.7 slice_multiply_fusion.refs_2_
  241.9 40.0 %sweep1.1 = (f32[8,8192]{1,0:T(8,128)}, f32[8,16384]{1,0:T(8,128)}, f32[1,8,512]{2,1,0:T(8,128)}) custom-call(s32[512]{0:T(512)} %select_reduce_fusion.2.ids, s32[1]{0:T(128)} %bitcast.1.count, f32[8,16384]{1,0:T(8,128)} %get-tuple-element.23.refs_0_, f32[16,16384]{1,0:T(8,128)} %exponential_select_fusion.refs_1_.refs_2_, ...), custom_call_target="tpu_custom_call" | custom-call | flops 864026624 | bytes 54001664 | tf_op jit(solution)/shard_map/sweep1/pallas_call | solution.py:344
  281.9 1.3 reduce_sum.171
  283.2 1.2 multiply_reduce_fusion.1
  284.5 1.9 pad_maximum_fusion.1.behind
  286.4 0.7 pad_maximum_fusion.4.ahead
  287.2 22.7 %exchange.3 = (f32[8,16384]{1,0:T(8,128)}, f32[8,8192]{1,0:T(8,128)}) custom-call(f32[4,8,2176]{2,1,0:T(8,128)} %pad_maximum_fusion.4.ahead, f32[8,8,2176]{2,1,0:T(8,128)} %pad_maximum_fusion.1.behind, f32[8,2048]{1,0:T(8,128)} %get-tuple-element.38.glow), custom_call_target="tpu_custom_call" | custom-call | tf_op jit(solution)/shard_map/exchange/pallas_call | solution.py:374
  309.9 1.0 slice_multiply_fusion.1
  310.8 0.8 pad_maximum_fusion.2.refs_3_
  311.7 40.5 %sweep2.1 = (f32[8,8192]{1,0:T(8,128)}, f32[8,16384]{1,0:T(8,128)}, f32[2,8,512]{2,1,0:T(8,128)}) custom-call(s32[512]{0:T(512)} %select_reduce_fusion.2.ids, s32[1]{0:T(128)} %bitcast.1.count, f32[8,16384]{1,0:T(8,128)} %get-tuple-element.27.refs_0_, f32[8,16384]{1,0:T(8,128)} %all_gather.31.refs_0_.refs_1_, ...), custom_call_target="tpu_custom_call" | custom-call | flops 864026624 | bytes 54001664 | tf_op jit(solution)/shard_map/sweep2/pallas_call | solution.py:344
  352.2 1.1 multiply_reduce_fusion
  353.3 0.8 constant_dynamic-update-slice_fusion
  354.1 0.1 reduce_sum.175
  354.2 1.3 reduce_sum.174
  355.5 0.6 select_maximum_fusion.value
  356.1 14.6 %totals.1 = f32[8,128]{1,0:T(8,128)} custom-call(f32[8,128]{1,0:T(8,128)} %select_maximum_fusion.value), custom_call_target="tpu_custom_call" | custom-call | tf_op jit(solution)/shard_map/totals/pallas_call | solution.py:425
  370.7 0.7 slice.51
  371.4 0.1 divide_reduce_fusion
  371.5 3.6 all-to-all-start
  375.2 0.1 select_reduce_fusion.4
  375.4 13.5 %all-gather.2 = f32[512,16]{0,1:T(8,128)S(1)} all-gather(f32[128,16]{0,1:T(8,128)S(1)} %select_reduce_fusion.4), channel_id=4, replica_groups=mesh['src'=4,'dst'=8] {'src'}, dimensions={0}, use_global_device_ids=true | all-gather | bytes 40960 | tf_op jit(solution)/shard_map/all_gather | solution.py:455
  388.9 0.8 multiply_bitcast_fusion
  389.7 0.7 collective-permute-start.2
  390.4 0.7 constant_dynamic-slice_fusion
  391.1 17.2 %all_gather.37 = f32[8,16384]{1,0:T(8,128)S(1)} all-gather(f32[8,2048]{1,0:T(8,128)S(1)} %collective-permute-done.2), channel_id=1, replica_groups=mesh['src'=4,'dst'=8] {'dst'}, dimensions={1}, use_global_device_ids=true | all-gather | bytes 589824 | tf_op jit(solution)/shard_map/all_gather | solution.py:446
  408.3 0.9 broadcast_divide_fusion
  409.2 1.3 bitcast_reduce_fusion
  410.5 0.8 multiply_divide_fusion
  (52 shorter events, 0.8 us)
Async XLA Ops:
  7.2 68.5 %copy-start = (bf16[8192,128]{1,0:T(8,128)(2,1)S(1)}, bf16[8192,128]{1,0:T(8,128)(2,1)}, u32[]{:S(2)}) copy-start(bf16[8192,128]{1,0:T(8,128)(2,1)} %param.11) | copy-start | bytes 6291460
  7.2 52.6 %copy-start.12 = (s32[3,8]{1,0:T(4,128)S(1)}, s32[3,8]{1,0:T(4,128)}, u32[]{:S(2)}) copy-start(s32[3,8]{1,0:T(4,128)} %param.15) | copy-start | bytes 292
  7.2 68.5 %copy-start.10 = (f32[8192]{0:T(1024)S(1)}, f32[8192]{0:T(1024)}, u32[]{:S(2)}) copy-start(f32[8192]{0:T(1024)} %param.13) | copy-start | bytes 98308
  7.2 69.7 %all-gather.9.cloned.1.call-start = ((), (), s32[]{:S(2)}) async-start(), calls=%async_computation.1 | async-start | bytes 4718592 | tf_op jit(solution)/shard_map/all_gather | solution.py:261
  8.5 0.7 collective-permute-start.1
  9.2 0.8 copy-start.6
  10.0 164.2 %all-gather.13.cloned.1.call-start = ((), (), s32[]{:S(2)}) async-start(), calls=%async_computation.3 | async-start | bytes 1179648 | tf_op jit(solution)/shard_map/all_gather | solution.py:331
  10.9 134.5 %collective-permute-start = (f32[8,2048]{1,0:T(8,128)S(1)}, f32[8,2048]{1,0:T(8,128)S(1)}, u32[]{:S(2)}, u32[]{:S(2)}) collective-permute-start(f32[8,2048]{1,0:T(8,128)S(1)} %constant_dynamic-slice_fusion.2), channel_id=1, source_target_pairs={{0,0},{4,1},{8,2},{12,3},{16,4},{20,5},{24,6},{28,7},{1,8},{5,9},{... | collective-permute-start | bytes 196616 | tf_op jit(solution)/shard_map/ppermute | solution.py:266
  57.9 1.4 copy-start.8
  139.9 1.6 copy-start.1
  139.9 4.1 copy-start.7
  144.0 265.2 %all-gather.11.cloned.1.call-start = ((), (), s32[]{:S(2)}) async-start(), calls=%async_computation.2 | async-start | bytes 1310720 | tf_op jit(solution)/shard_map/all_gather | solution.py:440
  174.3 3.7 copy-start.2
  212.2 4.5 %copy-start.5 = (f32[8,8192]{1,0:T(8,128)S(1)}, f32[8,8192]{1,0:T(8,128)}, u32[]{:S(2)}) copy-start(f32[8,8192]{1,0:T(8,128)} %get-tuple-element.21) | copy-start | bytes 786436
  281.9 4.6 %copy-start.4 = (f32[8,8192]{1,0:T(8,128)S(1)}, f32[8,8192]{1,0:T(8,128)}, u32[]{:S(2)}) copy-start(f32[8,8192]{1,0:T(8,128)} %get-tuple-element.25) | copy-start | bytes 786436
  283.2 27.6 %copy-start.3 = (f32[8,8192]{1,0:T(8,128)S(1)}, f32[8,8192]{1,0:T(8,128)}, u32[]{:S(2)}) copy-start(f32[8,8192]{1,0:T(8,128)} %slice_multiply_fusion.2.refs_2_) | copy-start | bytes 786436
  311.7 41.7 %copy-start.11 = (f32[1,8,512]{2,1,0:T(8,128)S(1)}, f32[1,8,512]{2,1,0:T(8,128)}, u32[]{:S(2)}) copy-start(f32[1,8,512]{2,1,0:T(8,128)} %get-tuple-element.31) | copy-start | bytes 49156
  352.2 23.1 %copy-start.9 = (pred[32,128]{1,0:T(8,128)(4,1)S(1)}, pred[32,128]{1,0:T(8,128)(4,1)}, u32[]{:S(2)}) copy-start(pred[32,128]{1,0:T(8,128)(4,1)} %copy-done.8) | copy-start | bytes 12292
  371.5 18.2 %all-to-all-start = ((f32[8,8,2048]{2,1,0:T(8,128)}), f32[8,8,2048]{2,1,0:T(8,128)S(1)}, u32[]{:S(2)}, u32[]{:S(2)}) async-start(f32[8,8,2048]{2,1,0:T(8,128)} %bitcast.60), calls=%async_computation | async-start | bytes 1048576 | tf_op jit(solution)/shard_map/all_to_all | solution.py:444
  389.7 1.4 collective-permute-start.2
Sparse Core Ops, SparseCore 0:
  10.5 66.2 all-gather.8
  144.1 30.1 all-gather.12
  353.4 32.9 all-gather.10
